TPU v7x, 512 devices: a whole 4x8x8 slice. The times are simulated.
512 devices in a mesh: space: 8 (over z_lo, core), frame: 64 (over z_hi, x, y).
Axes of the slice: x: 4, y: 8, z: 8 (z_hi: 2, z_lo: 4; z = z_hi * 4 + z_lo), core: 2. Of those that a mesh axis runs over, the one named last changes fastest.
Arguments:
- series: bfloat16 [512, 64, 32, 128], P('frame', 'space'), may hold values from -6 to 6
- offsets: int32 [8], P('space'), may hold values from 0 to 32767
Outputs:
- smoothed: float32 [512, 64, 32, 128], P('frame', 'space')
Inputs may be any that keep to these rules, and one draw needn't show every extreme that they name: `offsets`: one shift for each slab.
All inputs are finite; a program needn't handle non-finite values.
Results may differ from a plain program's by a relative error of at most 0.012.
The roundings to bfloat16 on the way count: a program that leaves them out, or rounds other values in their place, can miss the bound.
Values may be sent and summed in bfloat16 or wider, within the bound.
No kernel may reach another device: no remote copies, remote signals or barrier semaphores. Data moves between devices by JAX's collectives and lax.ppermute only.
A program may use at most 64 MiB of HBM per device.

v0:
```python
import jax
import jax.numpy as jnp
from jax import lax
from jax.sharding import PartitionSpec as P

ITERS = 6


smooth_rate = 0.12


def padded_2(shard, sides, width):
    for axis, dim in sides:
        count, length = (lax.axis_size(axis), shard.shape[dim])
        up = [(i, (i + 1) % count) for i in range(count - 1)]
        down = [(j, i) for i, j in up]
        last = lax.slice_in_dim(shard, length - width, length, axis=dim)
        initial = lax.slice_in_dim(shard, 0, width, axis=dim)
        before = lax.ppermute(last, axis, up)
        after = lax.ppermute(initial, axis, down)
        shard = jnp.concatenate([before, shard, after], axis=dim)
    return shard


def shrink_block(block):
    size = block.shape[0]
    total = jnp.sum(jnp.square(block.astype(jnp.float32)))
    gram = jnp.dot(block, block.T, preferred_element_type=jnp.float32) * (size / (total + 1e-06))
    norm_gram = jnp.sqrt(jnp.sum(gram * gram))
    identity = jnp.eye(size, dtype=jnp.float32)
    shifted = (gram + identity).astype(jnp.bfloat16)
    inverse = (identity / (1.0 + norm_gram)).astype(jnp.bfloat16)
    for _ in range(ITERS):
        product = jnp.dot(shifted, inverse, preferred_element_type=jnp.float32).astype(jnp.bfloat16)
        inverse = (
            2.0 * inverse.astype(jnp.float32)
            - jnp.dot(inverse, product, preferred_element_type=jnp.float32)
        ).astype(jnp.bfloat16)
    mixing = jnp.dot(gram.astype(jnp.bfloat16), inverse, preferred_element_type=jnp.float32).astype(
        jnp.bfloat16
    )
    result = lax.dot_general(
        mixing, block, (((0,), (0,)), ((), ())), preferred_element_type=jnp.float32
    )
    return result.astype(jnp.bfloat16)


def on_device(series, offsets):
    frames_local, width_x, width_y, width_z = series.shape
    voxel_count = width_x * width_y * width_z
    frame_devices = lax.axis_size("frame")
    block_voxels = voxel_count // frame_devices
    offset_now = offsets[0]
    flat = series.reshape(frames_local, voxel_count)
    doubled = jnp.concatenate([flat, flat], axis=1)
    rolled = lax.dynamic_slice_in_dim(doubled, offset_now, voxel_count, 1)
    outgoing = rolled.reshape(frames_local, frame_devices, block_voxels)
    arrived = lax.all_to_all(outgoing, "frame", split_axis=1, concat_axis=0, tiled=True)
    block = arrived.reshape(frames_local * frame_devices, block_voxels)
    shrunk = shrink_block(block)
    returning = shrunk.reshape(frame_devices, frames_local, block_voxels)
    undo_offset = (voxel_count - offset_now) % voxel_count
    received = lax.all_to_all(returning, "frame", split_axis=0, concat_axis=2, tiled=True)
    count = received.shape[1]
    flat_back = received.reshape(count, voxel_count)
    twice = jnp.concatenate([flat_back, flat_back], axis=1)
    restored = lax.dynamic_slice_in_dim(twice, undo_offset, voxel_count, 1)
    restored = restored.reshape(count, width_x, width_y, width_z)
    extended = padded_2(restored, (("space", 1),), 1)
    padded = jnp.pad(extended.astype(jnp.float32), ((0, 0), (0, 0), (1, 1), (1, 1)))
    centre = padded[:, 1:-1, 1:-1, 1:-1]
    beside = padded[:, 2:, 1:-1, 1:-1] + padded[:, :-2, 1:-1, 1:-1]
    beside = beside + padded[:, 1:-1, 2:, 1:-1] + padded[:, 1:-1, :-2, 1:-1]
    beside = beside + padded[:, 1:-1, 1:-1, 2:] + padded[:, 1:-1, 1:-1, :-2]
    return (1.0 - 6.0 * smooth_rate) * centre + smooth_rate * beside


def solution(mesh):
    in_specs = (P("frame", "space", None, None), P("space"))
    out_specs = P("frame", "space", None, None)
    return jax.shard_map(
        on_device, mesh=mesh, in_specs=in_specs, out_specs=out_specs, check_vma=False
    )
```

profile of v0, /device:TPU:1, one launch (start us, length us, event | category | flops | bytes accessed | tf_op | source)
XLA Modules:
  0.0 96.0 jit_solution(18336016425690024127)
XLA Ops:
  0.7 1.4 %copy.6 = bf16[1,8,256,128]{3,1,2,0:T(8,128)(2,1)S(1)} copy(bf16[1,8,256,128]{3,2,1,0:T(8,128)(2,1)} %bitcast.58) | data formatting | bytes 1048576
  2.0 2.0 %fusion.17 = bf16[8,32768]{1,0:T(8,128)(2,1)S(1)} fusion(s32[]{:T(128)S(6)} %select_n.13, bf16[8,32768]{1,0:T(8,128)(2,1)S(1)} %bitcast.56), kind=kLoop, calls=%fused_computation.48 | loop fusion | flops 1048576 | bytes 1048580 | tf_op jit(solution)/shard_map/concatenate | solution.py:55
  4.1 40.1 %all_to_all.30 = bf16[8,64,512]{2,0,1:T(8,128)(2,1)S(1)} all-to-all(bf16[8,64,512]{2,0,1:T(8,128)(2,1)S(1)} %bitcast.57), channel_id=1, replica_groups=mesh['space'=8,'frame'=64] {'frame'}, dimensions={1} | all-to-all | bytes 1048576 | tf_op jit(solution)/shard_map/all_to_all | solution.py:58
  44.1 0.9 multiply_reduce_fusion.1
  45.7 1.2 %multiply_reduce_fusion = (f32[]{:T(128)}, bf16[512,512]{1,0:T(8,128)(2,1)S(1)}, bf16[512,512]{1,0:T(8,128)(2,1)S(1)}) fusion(f32[]{:T(128)S(6)} %div.9, bf16[8,64,512]{2,0,1:T(8,128)(2,1)S(1)} %all_to_all.30), kind=kOutput, calls=%fused_computation.42 | convolution fusion | flops 270532608 | bytes 1572872 | tf_op jit(solution)/shard_map/dot_general | solution.py:28
  47.7 0.8 fusion
  48.4 0.8 fusion.1
  49.2 0.8 fusion.2
  50.0 0.8 fusion.3
  50.8 0.8 fusion.4
  51.6 0.4 convolution_convert_fusion.2
  52.0 0.8 convolution_convert_fusion.1
  52.8 1.3 %fusion.6 = bf16[64,8,512]{2,1,0:T(8,128)(2,1)} fusion(bf16[512,512]{1,0:T(8,128)(2,1)S(1)} %convolution_convert_fusion.1, bf16[8,64,512]{2,0,1:T(8,128)(2,1)S(1)} %all_to_all.30), kind=kOutput, calls=%fused_computation.25 | convolution fusion | flops 268697600 | bytes 1572864 | tf_op jit(solution)/shard_map/dot_general | solution.py:42
  54.1 6.3 %all-to-all-start.1 = ((bf16[64,8,512]{2,1,0:T(8,128)(2,1)}), bf16[64,8,512]{2,1,0:T(8,128)(2,1)S(1)}, u32[]{:S(2)}, u32[]{:S(2)}) async-start(bf16[64,8,512]{2,1,0:T(8,128)(2,1)} %fusion.6), calls=%async_computation.1 | async-start | bytes 1048576 | tf_op jit(solution)/shard_map/all_to_all | solution.py:63
  60.4 19.8 %all-to-all-done.1 = bf16[64,8,512]{2,1,0:T(8,128)(2,1)S(1)} async-done(((bf16[64,8,512]{2,1,0:T(8,128)(2,1)}), bf16[64,8,512]{2,1,0:T(8,128)(2,1)S(1)}, u32[]{:S(2)}, u32[]{:S(2)}) %all-to-all-start.1) | async-done | bytes 524320 | tf_op jit(solution)/shard_map/all_to_all | solution.py:63
  80.2 2.0 %fusion.16 = bf16[1,8,256,128]{3,1,2,0:T(8,128)(2,1)S(1)} fusion(s32[]{:T(128)S(6)} %select_n.15, bf16[8,32768]{1,0:T(8,128)(2,1)S(1)} %bitcast.55), kind=kLoop, calls=%fused_computation.47 | loop fusion | flops 1048576 | bytes 1048580
  82.3 0.1 copy.4
  82.3 6.4 %collective-permute-start = (bf16[8,1,32,128]{3,2,1,0:T(8,128)(2,1)S(1)}, bf16[8,1,32,128]{3,2,1,0:T(8,128)(2,1)S(1)}, u32[]{:S(2)}, u32[]{:S(2)}) collective-permute-start(bf16[8,1,32,128]{3,2,1,0:T(8,128)(2,1)S(1)} %get-tuple-element.7), channel_id=1, source_target_pairs={{0,64},{64,128},{128,192},{192,256},{256,320},{320,384},{384,448},... | collective-permute-start | bytes 196616 | tf_op jit(solution)/shard_map/ppermute | solution.py:19
  88.7 1.9 %collective-permute-start.1 = (bf16[8,1,32,128]{3,2,1,0:T(8,128)(2,1)S(1)}, bf16[8,1,32,128]{3,2,1,0:T(8,128)(2,1)S(1)}, u32[]{:S(2)}, u32[]{:S(2)}) collective-permute-start(bf16[8,1,32,128]{3,2,1,0:T(8,128)(2,1)S(1)} %get-tuple-element.8), channel_id=1, source_target_pairs={{64,0},{128,64},{192,128},{256,192},{320,256},{384,320},{448,384},... | collective-permute-start | bytes 196616 | tf_op jit(solution)/shard_map/ppermute | solution.py:20
  90.7 0.0 collective-permute-done
  90.7 3.6 %collective-permute-done.1 = bf16[8,1,32,128]{3,2,1,0:T(8,128)(2,1)S(1)} collective-permute-done((bf16[8,1,32,128]{3,2,1,0:T(8,128)(2,1)S(1)}, bf16[8,1,32,128]{3,2,1,0:T(8,128)(2,1)S(1)}, u32[]{:S(2)}, u32[]{:S(2)}) %collective-permute-start.1) | collective-permute-done | bytes 65568 | tf_op jit(solution)/shard_map/ppermute | solution.py:20
  94.3 0.1 maximum_convert_fusion
  94.4 1.6 %fusion.12 = f32[8,8,32,128]{3,2,1,0:T(8,128)} fusion(f32[8,10,32,128]{3,2,1,0:T(8,128)S(1)} %maximum_convert_fusion), kind=kLoop, calls=%fused_computation.31 | loop fusion | flops 2097152 | bytes 5505024 | tf_op jit(solution)/shard_map/add | solution.py:75
  (1 shorter events, 0.0 us)
Async XLA Ops:
  54.1 26.2 %all-to-all-start.1 = ((bf16[64,8,512]{2,1,0:T(8,128)(2,1)}), bf16[64,8,512]{2,1,0:T(8,128)(2,1)S(1)}, u32[]{:S(2)}, u32[]{:S(2)}) async-start(bf16[64,8,512]{2,1,0:T(8,128)(2,1)} %fusion.6), calls=%async_computation.1 | async-start | bytes 1048576 | tf_op jit(solution)/shard_map/all_to_all | solution.py:63
  82.3 8.3 %collective-permute-start = (bf16[8,1,32,128]{3,2,1,0:T(8,128)(2,1)S(1)}, bf16[8,1,32,128]{3,2,1,0:T(8,128)(2,1)S(1)}, u32[]{:S(2)}, u32[]{:S(2)}) collective-permute-start(bf16[8,1,32,128]{3,2,1,0:T(8,128)(2,1)S(1)} %get-tuple-element.7), channel_id=1, source_target_pairs={{0,64},{64,128},{128,192},{192,256},{256,320},{320,384},{384,448},... | collective-permute-start | bytes 196616 | tf_op jit(solution)/shard_map/ppermute | solution.py:19
  88.7 5.6 %collective-permute-start.1 = (bf16[8,1,32,128]{3,2,1,0:T(8,128)(2,1)S(1)}, bf16[8,1,32,128]{3,2,1,0:T(8,128)(2,1)S(1)}, u32[]{:S(2)}, u32[]{:S(2)}) collective-permute-start(bf16[8,1,32,128]{3,2,1,0:T(8,128)(2,1)S(1)} %get-tuple-element.8), channel_id=1, source_target_pairs={{64,0},{128,64},{192,128},{256,192},{320,256},{384,320},{448,384},... | collective-permute-start | bytes 196616 | tf_op jit(solution)/shard_map/ppermute | solution.py:20
where the time goes:
time: 96.3 us; the launch traced here: 96 us
  blocking collectives  40.1 us (42%)
  waiting for transfers between devices  23.5 us (24%)
  starting transfers between devices  14.6 us (15%)
  matrix products  7.57 us (8%)
  other arithmetic  6.62 us (7%)
  between operations  2.2 us (2%)
  local copies, waits for them, and re-layouts  1.47 us (2%)
    all_to_all x1, blocking collectives, on_device(): lax.all_to_all(outgoing, 'frame', split_axis=1, concat_axis=0, tiled=True)  40.1 us
    all_to_all x1, waiting for transfers between devices, on_device(): lax.all_to_all(returning, 'frame', split_axis=0, concat_axis=2, tiled=True)  19.8 us
    ppermute x1, starting transfers between devices, padded_2(): before = lax.ppermute(last, axis, up)  6.39 us
    all_to_all x1, starting transfers between devices, on_device(): lax.all_to_all(returning, 'frame', split_axis=0, concat_axis=2, tiled=True)  6.3 us
    dot_general x5, matrix products, shrink_block(): jnp.dot(inverse, product, preferred_element_type=jnp.float32)  3.89 us
    ppermute x1, waiting for transfers between devices, padded_2(): after = lax.ppermute(initial, axis, down)  3.65 us
    concatenate x1, other arithmetic, on_device(): doubled = jnp.concatenate([flat, flat], axis=1)  2.04 us
    unnamed x1, other arithmetic  2.03 us
  transfers between devices with their start and end apart: 3, of which 2 were waited for; matrix products, arithmetic and copies ran while one was open for 0% of the time, Pallas kernels for 0%

commit v1 on v0

v1 whole, which is shorter than its diff:
```python
import jax
import jax.numpy as jnp
from jax import lax
from jax.experimental import pallas as pl
from jax.experimental.pallas import tpu as pltpu
from jax.sharding import PartitionSpec as P
ITERS=6
RATE=0.12
F32=jnp.float32; BF=jnp.bfloat16
VM=pl.BlockSpec(memory_space=pltpu.VMEM); SM=pl.BlockSpec(memory_space=pltpu.SMEM); ANY=pl.BlockSpec(memory_space=pl.ANY)

def spread_kernel(off_ref, x_ref, o_ref, s_ref):
    sh = off_ref[0] & 511
    rr = sh >> 7
    lr = sh & 127
    for f in range(8):
        v = x_ref[f].astype(F32)
        s_ref[pl.ds(f, 256, stride=8), :] = v
    s_ref[2048:2088, :] = s_ref[0:40, :]
    lane = lax.broadcasted_iota(jnp.int32, (8,128), 1)
    keep = lane < 128 - lr
    back = (128 - lr) & 127
    def row(R):
        return pltpu.roll(s_ref[pl.ds(pl.multiple_of((rr+R)*8,8),8),:], back, 1)
    for j in range(0,64,2):
        rows=[row(4*j+i) for i in range(9)]
        o=[jnp.where(keep, rows[i], rows[i+1]) for i in range(8)]
        for c in range(4):
            o_ref[j,:,c*128:(c+1)*128]=o[c].astype(BF)
            o_ref[j+1,:,c*128:(c+1)*128]=o[4+c].astype(BF)

def spread(off,x):
    return pl.pallas_call(spread_kernel, out_shape=jax.ShapeDtypeStruct((64,8,512),BF),
        in_specs=[SM,VM], out_specs=VM, scratch_shapes=[pltpu.VMEM((2088,128),F32)], name="spread",
        cost_estimate=pl.CostEstimate(flops=1<<20,bytes_accessed=1<<20,transcendentals=0))(off,x)

def shrink_kernel(m_ref, y_ref, a_ref, g_ref, w_ref, z_ref):
    n=512
    m=m_ref[...]
    gram=lax.dot_general(m,m,(((1,),(1,)),((),())),preferred_element_type=F32)
    eye=lax.broadcasted_iota(jnp.int32,(n,n),0)==lax.broadcasted_iota(jnp.int32,(n,n),1)
    total=jnp.sum(jnp.where(eye,gram,0.0))
    g=gram*(n/(total+1e-6))
    norm=jnp.sqrt(jnp.sum(g*g))
    idn=jnp.where(eye,1.0,0.0)
    a=(g+idn).astype(BF)
    a_ref[...]=a
    g_ref[...]=g.astype(BF)
    c=(1.0/(1.0+norm)).astype(BF).astype(F32)
    w=(a.astype(F32)*c).astype(BF).astype(F32)
    z_ref[...]=(jnp.where(eye,2.0*c,0.0)-c*w).astype(BF)
    def step(_,carry):
        w_ref[...]=jnp.dot(z_ref[...],a_ref[...],preferred_element_type=F32).astype(BF)
        z=z_ref[...]
        z_ref[...]=(2.0*z.astype(F32)-jnp.dot(w_ref[...],z,preferred_element_type=F32)).astype(BF)
        return carry
    lax.fori_loop(0,ITERS-1,step,0)
    w_ref[...]=jnp.dot(z_ref[...],g_ref[...],preferred_element_type=F32).astype(BF)
    y_ref[...]=jnp.dot(w_ref[...],m_ref[...],preferred_element_type=F32).astype(BF)

def shrink(m):
    sc=[pltpu.VMEM((512,512),BF)]*4
    return pl.pallas_call(shrink_kernel,out_shape=jax.ShapeDtypeStruct((512,512),BF),in_specs=[VM],out_specs=VM,scratch_shapes=sc,name="shrink",
        cost_estimate=pl.CostEstimate(flops=13*2*512**3,bytes_accessed=1<<20,transcendentals=0))(m)

def _unshift_rows(y_ref, t_ref, lr, chunks, base):
    for j in chunks:
        v = y_ref[j].astype(F32)
        for c in range(4):
            t_ref[base + 4*j + c] = pltpu.roll(v[:, c*128:(c+1)*128], lr, 1)

def edges_kernel(off_ref, y_ref, first_ref, last_ref, t_ref):
    sh = off_ref[0] & 511
    rr = sh >> 7
    lr = sh & 127
    lane = lax.broadcasted_iota(jnp.int32, (8,128), 1)
    keep = lane >= lr
    for k,j in enumerate([63]+list(range(8))):
        v = y_ref[j].astype(F32)
        for c in range(4):
            t_ref[4*k + c] = pltpu.roll(v[:, c*128:(c+1)*128], lr, 1)
    prev = t_ref[3 - rr]
    for R in range(32):
        cur = t_ref[R + 4 - rr]
        first_ref[R] = jnp.where(keep, cur, prev).astype(BF)
        prev = cur
    for k,j in enumerate(range(55,64)):
        v = y_ref[j].astype(F32)
        for c in range(4):
            t_ref[4*k + c] = pltpu.roll(v[:, c*128:(c+1)*128], lr, 1)
    prev = t_ref[3 - rr]
    for R in range(32):
        cur = t_ref[R + 4 - rr]
        last_ref[R] = jnp.where(keep, cur, prev).astype(BF)
        prev = cur

def edges(off,y):
    s=jax.ShapeDtypeStruct((32,8,128),BF)
    return pl.pallas_call(edges_kernel,out_shape=(s,s),in_specs=[SM,VM],out_specs=(VM,VM),scratch_shapes=[pltpu.VMEM((36,8,128),F32)],name="edges",
        cost_estimate=pl.CostEstimate(flops=1<<16,bytes_accessed=1<<18,transcendentals=0))(off,y)

def inner_kernel(off_ref, y_ref, out_ref, part_ref, t_ref, u_ref, o_ref, sem):
    sh = off_ref[0] & 511
    rr = sh >> 7
    lr = sh & 127
    lane = lax.broadcasted_iota(jnp.int32, (8,128), 1)
    keep = lane >= lr
    for j in [63]+list(range(64)):
        v = y_ref[j].astype(F32)
        base = 0 if j==63 else 4
        for c in range(4):
            val = pltpu.roll(v[:, c*128:(c+1)*128], lr, 1)
            if j==63: t_ref[260-4 + c] = val
            else: t_ref[4 + 4*j + c] = val
    t_ref[0:4] = t_ref[256:260]
    prev = t_ref[3 - rr]
    for R in range(256):
        cur = t_ref[R + 4 - rr]
        u_ref[R] = jnp.where(keep, cur, prev)
        prev = cur
    lo = lane > 0
    hi = lane < 127
    for p in range(8):
        for y in range(32):
            R = p*32+y
            c = u_ref[R]
            s = jnp.where(hi, pltpu.roll(c,127,1), 0.0) + jnp.where(lo, pltpu.roll(c,1,1), 0.0)
            if y>0: s = s + u_ref[R-1]
            if y<31: s = s + u_ref[R+1]
            if p>0: s = s + u_ref[R-32]
            if p<7: s = s + u_ref[R+32]
            val = (1.0-6.0*RATE)*c + RATE*s
            if p in (0,7): part_ref[0 if p==0 else 1, :, y, :] = val
            else: o_ref[p-1, :, y, :] = val
        if p not in (0,7):
            pltpu.make_async_copy(o_ref.at[p-1], out_ref.at[:,p], sem.at[p-1]).start()
    for p in range(6):
        pltpu.make_async_copy(o_ref.at[p], out_ref.at[:,p+1], sem.at[p]).wait()

def inner(off,y):
    return pl.pallas_call(inner_kernel,out_shape=(jax.ShapeDtypeStruct((8,8,32,128),F32),jax.ShapeDtypeStruct((2,8,32,128),F32)),
        in_specs=[SM,VM],out_specs=(ANY,VM),scratch_shapes=[pltpu.VMEM((260,8,128),F32),pltpu.VMEM((256,8,128),F32),pltpu.VMEM((6,8,32,128),F32),pltpu.SemaphoreType.DMA((6,))],name="inner",
        cost_estimate=pl.CostEstimate(flops=1<<22,bytes_accessed=3<<19,transcendentals=0))(off,y)

def halo_kernel(lo_ref, hi_ref, part_ref, in_ref, out_ref, o_ref, sem):
    for k,h in ((0,lo_ref),(1,hi_ref)):
        for y in range(32):
            o_ref[k,:,y,:] = part_ref[k,:,y,:] + RATE*h[y].astype(F32)
        pltpu.make_async_copy(o_ref.at[k], out_ref.at[:,7*k], sem.at[k]).start()
    for k in range(2):
        pltpu.make_async_copy(o_ref.at[k], out_ref.at[:,7*k], sem.at[k]).wait()

def halo(lo,hi,part,out):
    return pl.pallas_call(halo_kernel,out_shape=jax.ShapeDtypeStruct((8,8,32,128),F32),in_specs=[VM,VM,VM,ANY],out_specs=ANY,
        scratch_shapes=[pltpu.VMEM((2,8,32,128),F32),pltpu.SemaphoreType.DMA((2,))],input_output_aliases={3:0},name="halo",
        cost_estimate=pl.CostEstimate(flops=1<<17,bytes_accessed=1<<19,transcendentals=0))(lo,hi,part,out)


def on_device(series, offsets):
    sent = spread(offsets, series.reshape(8, 256, 128))
    arrived = lax.all_to_all(sent, "frame", split_axis=0, concat_axis=0, tiled=True)
    shrunk = shrink(arrived.reshape(512, 512))
    back = lax.all_to_all(shrunk.reshape(64, 8, 512), "frame", split_axis=0, concat_axis=0, tiled=True)
    first, last = edges(offsets, back)
    count = lax.axis_size("space")
    up = [(i, i + 1) for i in range(count - 1)]
    down = [(j, i) for i, j in up]
    before = lax.ppermute(last, "space", up)
    after = lax.ppermute(first, "space", down)
    out, part = inner(offsets, back)
    return halo(before, after, part, out)


def solution(mesh):
    in_specs = (P("frame", "space", None, None), P("space"))
    out_specs = P("frame", "space", None, None)
    return jax.shard_map(
        on_device, mesh=mesh, in_specs=in_specs, out_specs=out_specs, check_vma=False
    )
```

time: 96.3 us -> 94.3 us (0.979)
  blocking collectives: 40.1 us -> 66 us
  waiting for transfers between devices: 23.5 us -> 0.22 us
  Pallas kernels: 0 us -> 17.4 us
  matrix products: 7.57 us -> 0 us
  other arithmetic: 6.62 us -> 0 us
  starting transfers between devices: 14.6 us -> 8.87 us
  between operations: 2.2 us -> 0.7 us
    all_to_all x1 -> x2, blocking collectives: 40.1 us -> 66 us  [the longest x1 40.4 us: on_device(): lax.all_to_all(sent, 'frame', split_axis=0, concat_axis=0, tiled=True)]
    all_to_all x1 -> x0, waiting for transfers between devices: 19.8 us -> none  [on_device(): lax.all_to_all(returning, 'frame', split_axis=0, concat_axis=2, tiled=True)]
    pallas_call x0 -> x5, Pallas kernels: none -> 17.4 us  [the longest x1 7.72 us: shrink(): pl.pallas_call(shrink_kernel, out_shape=jax.ShapeDtypeStruct((512, 512),...]
    dot_general x9 -> x0, matrix products: 7.57 us -> none  [the longest x5 3.89 us: shrink_block(): jnp.dot(inverse, product, preferred_element_type=jnp.float32)]
    all_to_all x1 -> x0, starting transfers between devices: 6.3 us -> none  [on_device(): lax.all_to_all(returning, 'frame', split_axis=0, concat_axis=2, tiled=True)]
    ppermute x2, waiting for transfers between devices: 3.65 us -> 0.22 us  [the longest x1 0.22 us: on_device(): after = lax.ppermute(first, 'space', down)]
    concatenate x1 -> x0, other arithmetic: 2.04 us -> none  [on_device(): doubled = jnp.concatenate([flat, flat], axis=1)]
    unnamed x1 -> x0, other arithmetic: 2.03 us -> none
  transfers between devices with their start and end apart: 3 -> 2, of which waited for: 2 -> 1; matrix products, arithmetic and copies ran while one was open for 0% -> 0% of each run, Pallas kernels for 0% -> 4%
where the time goes in v1:
time: 94.3 us; the launch traced here: 93.8 us
  blocking collectives  66 us (70%)
  Pallas kernels  17.4 us (18%)
  starting transfers between devices  8.87 us (9%)
    all_to_all x1, blocking collectives, on_device(): lax.all_to_all(sent, 'frame', split_axis=0, concat_axis=0, tiled=True)  40.4 us
    all_to_all x1, blocking collectives, on_device(): lax.all_to_all(shrunk.reshape(64, 8, 512), 'frame', split_axis=0, concat_...  25.6 us
    pallas_call x1, Pallas kernels, shrink(): pl.pallas_call(shrink_kernel, out_shape=jax.ShapeDtypeStruct((512, 512),...  7.72 us
    ppermute x1, starting transfers between devices, on_device(): before = lax.ppermute(last, 'space', up)  6.95 us
    pallas_call x1, Pallas kernels, inner(): pl.pallas_call(inner_kernel, out_shape=(jax.ShapeDtypeStruct((8, 8, 32, 1...  3.62 us
    pallas_call x1, Pallas kernels, spread(): pl.pallas_call(spread_kernel, out_shape=jax.ShapeDtypeStruct((64, 8, 512)...  2.22 us
    pallas_call x1, Pallas kernels, halo(): pl.pallas_call(halo_kernel, out_shape=jax.ShapeDtypeStruct((8, 8, 32, 128...  1.99 us
    ppermute x1, starting transfers between devices, on_device(): after = lax.ppermute(first, 'space', down)  1.92 us
  transfers between devices with their start and end apart: 2, of which 1 were waited for; matrix products, arithmetic and copies ran while one was open for 0% of the time, Pallas kernels for 4%

profile of v1, /device:TPU:1, one launch (start us, length us, event | category | flops | bytes accessed | tf_op | source)
XLA Modules:
  0.0 93.8 jit_solution(8059522667044267649)
XLA Ops:
  0.7 2.2 %spread.1 = bf16[64,8,512]{2,1,0:T(8,128)(2,1)} custom-call(s32[1]{0:T(128)S(6)} %copy.5.off_ref, bf16[8,256,128]{2,1,0:T(8,128)(2,1)} %bitcast.5), custom_call_target="tpu_custom_call" | custom-call | flops 1048576 | bytes 1048576 | tf_op jit(solution)/shard_map/spread/pallas_call | solution.py:33
  2.9 40.4 %all_to_all.10 = bf16[64,8,512]{2,1,0:T(8,128)(2,1)} all-to-all(bf16[64,8,512]{2,1,0:T(8,128)(2,1)} %spread.1), channel_id=1, replica_groups=mesh['space'=8,'frame'=64] {'frame'}, dimensions={0} | all-to-all | bytes 1048576 | tf_op jit(solution)/shard_map/all_to_all | solution.py:161
  43.2 7.7 %shrink.1 = bf16[512,512]{1,0:T(8,128)(2,1)} custom-call(bf16[512,512]{1,0:T(8,128)(2,1)} %bitcast.3), custom_call_target="tpu_custom_call" | custom-call | flops 3489660928 | bytes 1048576 | tf_op jit(solution)/shard_map/shrink/pallas_call | solution.py:63
  51.0 25.6 %all_to_all.11.y_ref = bf16[64,8,512]{2,1,0:T(8,128)(2,1)} all-to-all(bf16[64,8,512]{2,1,0:T(8,128)(2,1)} %bitcast.4), channel_id=1, replica_groups=mesh['space'=8,'frame'=64] {'frame'}, dimensions={0} | all-to-all | bytes 1048576 | tf_op jit(solution)/shard_map/all_to_all | solution.py:163
  76.6 1.8 %edges.1 = (bf16[32,8,128]{2,1,0:T(8,128)(2,1)}, bf16[32,8,128]{2,1,0:T(8,128)(2,1)}) custom-call(s32[1]{0:T(128)S(6)} %copy.5.off_ref, bf16[64,8,512]{2,1,0:T(8,128)(2,1)} %all_to_all.11.y_ref), custom_call_target="tpu_custom_call" | custom-call | flops 65536 | bytes 262144 | tf_op jit(solution)/shard_map/edges/pallas_call | solution.py:99
  78.4 7.0 %collective-permute-start = (bf16[32,8,128]{2,1,0:T(8,128)(2,1)}, bf16[32,8,128]{2,1,0:T(8,128)(2,1)S(1)}, u32[]{:S(2)}, u32[]{:S(2)}) collective-permute-start(bf16[32,8,128]{2,1,0:T(8,128)(2,1)} %get-tuple-element.9), channel_id=1, source_target_pairs={{0,64},{64,128},{128,192},{192,256},{256,320},{320,384},{384,448},... | collective-permute-start | bytes 196616 | tf_op jit(solution)/shard_map/ppermute | solution.py:168
  85.4 1.9 %collective-permute-start.1 = (bf16[32,8,128]{2,1,0:T(8,128)(2,1)}, bf16[32,8,128]{2,1,0:T(8,128)(2,1)S(1)}, u32[]{:S(2)}, u32[]{:S(2)}) collective-permute-start(bf16[32,8,128]{2,1,0:T(8,128)(2,1)} %get-tuple-element.10), channel_id=1, source_target_pairs={{64,0},{128,64},{192,128},{256,192},{320,256},{384,320},{448,384},... | collective-permute-start | bytes 196616 | tf_op jit(solution)/shard_map/ppermute | solution.py:169
  87.3 3.6 %inner.1 = (f32[8,8,32,128]{3,2,1,0:T(8,128)}, f32[2,8,32,128]{3,2,1,0:T(8,128)}) custom-call(s32[1]{0:T(128)S(6)} %copy.5.off_ref, bf16[64,8,512]{2,1,0:T(8,128)(2,1)} %all_to_all.11.y_ref), custom_call_target="tpu_custom_call" | custom-call | flops 4194304 | bytes 1572864 | tf_op jit(solution)/shard_map/inner/pallas_call | solution.py:141
  90.9 0.0 collective-permute-done.lo_ref
  90.9 0.0 copy-start
  90.9 0.2 collective-permute-done.1.hi_ref
  91.2 0.0 copy-start.1
  91.2 0.4 copy-done
  91.5 0.2 copy-done.1
  91.8 2.0 %halo.1 = f32[8,8,32,128]{3,2,1,0:T(8,128)} custom-call(bf16[32,8,128]{2,1,0:T(8,128)(2,1)} %copy-done, bf16[32,8,128]{2,1,0:T(8,128)(2,1)} %copy-done.1, f32[2,8,32,128]{3,2,1,0:T(8,128)} %get-tuple-element.11.part_ref, f32[8,8,32,128]{3,2,1,0:T(8,128)} %get-tuple-element.12.in_ref), custom_call_target="tpu_custom_call", output_to_operand_aliasing={{}: (3, {})} | custom-call | flops 131072 | bytes 524288 | tf_op jit(solution)/shard_map/halo/pallas_call | solution.py:154
Async XLA Ops:
  78.4 12.5 %collective-permute-start = (bf16[32,8,128]{2,1,0:T(8,128)(2,1)}, bf16[32,8,128]{2,1,0:T(8,128)(2,1)S(1)}, u32[]{:S(2)}, u32[]{:S(2)}) collective-permute-start(bf16[32,8,128]{2,1,0:T(8,128)(2,1)} %get-tuple-element.9), channel_id=1, source_target_pairs={{0,64},{64,128},{128,192},{192,256},{256,320},{320,384},{384,448},... | collective-permute-start | bytes 196616 | tf_op jit(solution)/shard_map/ppermute | solution.py:168
  85.4 5.8 %collective-permute-start.1 = (bf16[32,8,128]{2,1,0:T(8,128)(2,1)}, bf16[32,8,128]{2,1,0:T(8,128)(2,1)S(1)}, u32[]{:S(2)}, u32[]{:S(2)}) collective-permute-start(bf16[32,8,128]{2,1,0:T(8,128)(2,1)} %get-tuple-element.10), channel_id=1, source_target_pairs={{64,0},{128,64},{192,128},{256,192},{320,256},{384,320},{448,384},... | collective-permute-start | bytes 196616 | tf_op jit(solution)/shard_map/ppermute | solution.py:169
  90.9 0.6 copy-start
  91.2 0.6 copy-start.1

commit v2 on v1

--- a/solution.py
+++ b/solution.py
@@ -5,6 +5,8 @@
 from jax.experimental.pallas import tpu as pltpu
 from jax.sharding import PartitionSpec as P
 ITERS=6
+LIM=16<<20
+GROUPS=[[(i + 60) % 64 for i in range(64)]]
 RATE=0.12
 F32=jnp.float32; BF=jnp.bfloat16
 VM=pl.BlockSpec(memory_space=pltpu.VMEM); SM=pl.BlockSpec(memory_space=pltpu.SMEM); ANY=pl.BlockSpec(memory_space=pl.ANY)
@@ -32,6 +34,7 @@
 def spread(off,x):
     return pl.pallas_call(spread_kernel, out_shape=jax.ShapeDtypeStruct((64,8,512),BF),
         in_specs=[SM,VM], out_specs=VM, scratch_shapes=[pltpu.VMEM((2088,128),F32)], name="spread",
+        compiler_params=pltpu.CompilerParams(vmem_limit_bytes=LIM),
         cost_estimate=pl.CostEstimate(flops=1<<20,bytes_accessed=1<<20,transcendentals=0))(off,x)
 
 def shrink_kernel(m_ref, y_ref, a_ref, g_ref, w_ref, z_ref):
@@ -61,6 +64,7 @@
 def shrink(m):
     sc=[pltpu.VMEM((512,512),BF)]*4
     return pl.pallas_call(shrink_kernel,out_shape=jax.ShapeDtypeStruct((512,512),BF),in_specs=[VM],out_specs=VM,scratch_shapes=sc,name="shrink",
+        compiler_params=pltpu.CompilerParams(vmem_limit_bytes=LIM),
         cost_estimate=pl.CostEstimate(flops=13*2*512**3,bytes_accessed=1<<20,transcendentals=0))(m)
 
 def _unshift_rows(y_ref, t_ref, lr, chunks, base):
@@ -97,6 +101,7 @@
 def edges(off,y):
     s=jax.ShapeDtypeStruct((32,8,128),BF)
     return pl.pallas_call(edges_kernel,out_shape=(s,s),in_specs=[SM,VM],out_specs=(VM,VM),scratch_shapes=[pltpu.VMEM((36,8,128),F32)],name="edges",
+        compiler_params=pltpu.CompilerParams(vmem_limit_bytes=LIM),
         cost_estimate=pl.CostEstimate(flops=1<<16,bytes_accessed=1<<18,transcendentals=0))(off,y)
 
 def inner_kernel(off_ref, y_ref, out_ref, part_ref, t_ref, u_ref, o_ref, sem):
@@ -140,6 +145,7 @@
 def inner(off,y):
     return pl.pallas_call(inner_kernel,out_shape=(jax.ShapeDtypeStruct((8,8,32,128),F32),jax.ShapeDtypeStruct((2,8,32,128),F32)),
         in_specs=[SM,VM],out_specs=(ANY,VM),scratch_shapes=[pltpu.VMEM((260,8,128),F32),pltpu.VMEM((256,8,128),F32),pltpu.VMEM((6,8,32,128),F32),pltpu.SemaphoreType.DMA((6,))],name="inner",
+        compiler_params=pltpu.CompilerParams(vmem_limit_bytes=LIM),
         cost_estimate=pl.CostEstimate(flops=1<<22,bytes_accessed=3<<19,transcendentals=0))(off,y)
 
 def halo_kernel(lo_ref, hi_ref, part_ref, in_ref, out_ref, o_ref, sem):
@@ -153,14 +159,15 @@
 def halo(lo,hi,part,out):
     return pl.pallas_call(halo_kernel,out_shape=jax.ShapeDtypeStruct((8,8,32,128),F32),in_specs=[VM,VM,VM,ANY],out_specs=ANY,
         scratch_shapes=[pltpu.VMEM((2,8,32,128),F32),pltpu.SemaphoreType.DMA((2,))],input_output_aliases={3:0},name="halo",
+        compiler_params=pltpu.CompilerParams(vmem_limit_bytes=LIM),
         cost_estimate=pl.CostEstimate(flops=1<<17,bytes_accessed=1<<19,transcendentals=0))(lo,hi,part,out)
 
 
 def on_device(series, offsets):
     sent = spread(offsets, series.reshape(8, 256, 128))
-    arrived = lax.all_to_all(sent, "frame", split_axis=0, concat_axis=0, tiled=True)
+    arrived = lax.all_to_all(sent, "frame", split_axis=0, concat_axis=0, tiled=True, axis_index_groups=GROUPS)
     shrunk = shrink(arrived.reshape(512, 512))
-    back = lax.all_to_all(shrunk.reshape(64, 8, 512), "frame", split_axis=0, concat_axis=0, tiled=True)
+    back = lax.all_to_all(shrunk.reshape(64, 8, 512), "frame", split_axis=0, concat_axis=0, tiled=True, axis_index_groups=GROUPS)
     first, last = edges(offsets, back)
     count = lax.axis_size("space")
     up = [(i, i + 1) for i in range(count - 1)]

time: 94.3 us -> 78.7 us (0.83)
  Pallas kernels: 17.4 us -> 9.29 us
  blocking collectives: 66 us -> 58.4 us
  starting transfers between devices: 8.87 us -> 7.28 us
  waiting for transfers between devices: 0.22 us -> 1.74 us
    all_to_all x1, blocking collectives: 40.4 us -> 32.4 us  [on_device(): lax.all_to_all(sent, 'frame', split_axis=0, concat_axis=0, tiled=True, ax...]
    pallas_call x1, Pallas kernels: 7.72 us -> 5.89 us  [shrink(): pl.pallas_call(shrink_kernel, out_shape=jax.ShapeDtypeStruct((512, 512),...]
    pallas_call x1, Pallas kernels: 2.22 us -> 0.38 us  [spread(): pl.pallas_call(spread_kernel, out_shape=jax.ShapeDtypeStruct((64, 8, 512)...]
    pallas_call x1, Pallas kernels: 3.62 us -> 1.9 us  [inner(): pl.pallas_call(inner_kernel, out_shape=(jax.ShapeDtypeStruct((8, 8, 32, 1...]
    pallas_call x1, Pallas kernels: 1.84 us -> 0.16 us  [edges(): pl.pallas_call(edges_kernel, out_shape=(s, s), in_specs=[SM, VM], out_spe...]
    ppermute x1, starting transfers between devices: 6.95 us -> 5.36 us  [on_device(): before = lax.ppermute(last, 'space', up)]
    ppermute x1, waiting for transfers between devices: 0.22 us -> 1.74 us  [on_device(): after = lax.ppermute(first, 'space', down)]
    pallas_call x1, Pallas kernels: 1.99 us -> 0.97 us  [halo(): pl.pallas_call(halo_kernel, out_shape=jax.ShapeDtypeStruct((8, 8, 32, 128...]
  transfers between devices with their start and end apart: 2 -> 2, of which waited for: 1 -> 1; matrix products, arithmetic and copies ran while one was open for 0% -> 0% of each run, Pallas kernels for 4% -> 2%
where the time goes in v2:
time: 78.7 us; the launch traced here: 78.5 us
  blocking collectives  58.4 us (74%)
  Pallas kernels  9.29 us (12%)
  starting transfers between devices  7.28 us (9%)
  waiting for transfers between devices  1.74 us (2%)
  local copies, waits for them, and re-layouts  1.03 us (1%)
    all_to_all x1, blocking collectives, on_device(): lax.all_to_all(sent, 'frame', split_axis=0, concat_axis=0, tiled=True, ax...  32.4 us
    all_to_all x1, blocking collectives, on_device(): lax.all_to_all(shrunk.reshape(64, 8, 512), 'frame', split_axis=0, concat_...  26 us
    pallas_call x1, Pallas kernels, shrink(): pl.pallas_call(shrink_kernel, out_shape=jax.ShapeDtypeStruct((512, 512),...  5.89 us
    ppermute x1, starting transfers between devices, on_device(): before = lax.ppermute(last, 'space', up)  5.36 us
    ppermute x1, starting transfers between devices, on_device(): after = lax.ppermute(first, 'space', down)  1.92 us
    pallas_call x1, Pallas kernels, inner(): pl.pallas_call(inner_kernel, out_shape=(jax.ShapeDtypeStruct((8, 8, 32, 1...  1.9 us
    ppermute x1, waiting for transfers between devices, on_device(): after = lax.ppermute(first, 'space', down)  1.74 us
  transfers between devices with their start and end apart: 2, of which 1 were waited for; matrix products, arithmetic and copies ran while one was open for 0% of the time, Pallas kernels for 2%

profile of v2, /device:TPU:1, one launch (start us, length us, event | category | flops | bytes accessed | tf_op | source)
XLA Modules:
  0.0 78.5 jit_solution(15589381070305728787)
XLA Ops:
  0.7 0.0 copy-start
  0.7 1.0 %copy-done = bf16[8,8,32,128]{3,2,1,0:T(8,128)(2,1)S(1)} copy-done((bf16[8,8,32,128]{3,2,1,0:T(8,128)(2,1)S(1)}, bf16[8,8,32,128]{3,2,1,0:T(8,128)(2,1)}, u32[]{:S(2)}) %copy-start) | copy-done | bytes 524312
  1.7 0.4 spread.1
  2.1 32.4 %all_to_all.10 = bf16[64,8,512]{2,1,0:T(8,128)(2,1)S(1)} all-to-all(bf16[64,8,512]{2,1,0:T(8,128)(2,1)S(1)} %spread.1), channel_id=1, replica_groups={{60,61,62,63,0,1,2,3,4,5,6,7,8,9,10,11,12,13,14,15,16,17,18,19,20,21,22..., dimensions={0} | all-to-all | bytes 1048576 | tf_op jit(solution)/shard_map/all_to_all | solution.py:168
  34.5 5.9 %shrink.1 = bf16[512,512]{1,0:T(8,128)(2,1)S(1)} custom-call(bf16[512,512]{1,0:T(8,128)(2,1)S(1)} %bitcast.3), custom_call_target="tpu_custom_call" | custom-call | flops 3489660928 | bytes 1048576 | tf_op jit(solution)/shard_map/shrink/pallas_call | solution.py:66
  40.4 26.0 %all_to_all.11.y_ref = bf16[64,8,512]{2,1,0:T(8,128)(2,1)S(1)} all-to-all(bf16[64,8,512]{2,1,0:T(8,128)(2,1)S(1)} %bitcast.4), channel_id=1, replica_groups={{60,61,62,63,0,1,2,3,4,5,6,7,8,9,10,11,12,13,14,15,16,17,18,19,20,21,22..., dimensions={0} | all-to-all | bytes 1048576 | tf_op jit(solution)/shard_map/all_to_all | solution.py:170
  66.4 0.2 edges.1
  66.5 5.4 %collective-permute-start = (bf16[32,8,128]{2,1,0:T(8,128)(2,1)S(1)}, bf16[32,8,128]{2,1,0:T(8,128)(2,1)S(1)}, u32[]{:S(2)}, u32[]{:S(2)}) collective-permute-start(bf16[32,8,128]{2,1,0:T(8,128)(2,1)S(1)} %get-tuple-element.9), channel_id=1, source_target_pairs={{0,64},{64,128},{128,192},{192,256},{256,320},{320,384},{384,448},... | collective-permute-start | bytes 196616 | tf_op jit(solution)/shard_map/ppermute | solution.py:175
  71.9 1.9 %collective-permute-start.1 = (bf16[32,8,128]{2,1,0:T(8,128)(2,1)S(1)}, bf16[32,8,128]{2,1,0:T(8,128)(2,1)S(1)}, u32[]{:S(2)}, u32[]{:S(2)}) collective-permute-start(bf16[32,8,128]{2,1,0:T(8,128)(2,1)S(1)} %get-tuple-element.10), channel_id=1, source_target_pairs={{64,0},{128,64},{192,128},{256,192},{320,256},{384,320},{448,384},... | collective-permute-start | bytes 196616 | tf_op jit(solution)/shard_map/ppermute | solution.py:176
  73.8 1.9 %inner.1 = (f32[8,8,32,128]{3,2,1,0:T(8,128)}, f32[2,8,32,128]{3,2,1,0:T(8,128)S(1)}) custom-call(s32[1]{0:T(128)S(6)} %copy.5.off_ref, bf16[64,8,512]{2,1,0:T(8,128)(2,1)S(1)} %all_to_all.11.y_ref), custom_call_target="tpu_custom_call" | custom-call | flops 4194304 | bytes 1572864 | tf_op jit(solution)/shard_map/inner/pallas_call | solution.py:146
  75.7 0.0 collective-permute-done.lo_ref
  75.7 1.7 %collective-permute-done.1.hi_ref = bf16[32,8,128]{2,1,0:T(8,128)(2,1)S(1)} collective-permute-done((bf16[32,8,128]{2,1,0:T(8,128)(2,1)S(1)}, bf16[32,8,128]{2,1,0:T(8,128)(2,1)S(1)}, u32[]{:S(2)}, u32[]{:S(2)}) %collective-permute-start.1) | collective-permute-done | bytes 65568 | tf_op jit(solution)/shard_map/ppermute | solution.py:176
  77.5 1.0 %halo.1 = f32[8,8,32,128]{3,2,1,0:T(8,128)} custom-call(bf16[32,8,128]{2,1,0:T(8,128)(2,1)S(1)} %collective-permute-done.lo_ref, bf16[32,8,128]{2,1,0:T(8,128)(2,1)S(1)} %collective-permute-done.1.hi_ref, f32[2,8,32,128]{3,2,1,0:T(8,128)S(1)} %get-tuple-element.11.part_ref, f32[8,8,32,128]{3,2,1,0:T(8,128)} %get-tuple-element.12.in_ref), custom_call_target="tpu_custom_call", output_to_operand_aliasing={{}: (3, {})} | custom-call | flops 131072 | bytes 524288 | tf_op jit(solution)/shard_map/halo/pallas_call | solution.py:160
Async XLA Ops:
  0.7 1.0 %copy-start = (bf16[8,8,32,128]{3,2,1,0:T(8,128)(2,1)S(1)}, bf16[8,8,32,128]{3,2,1,0:T(8,128)(2,1)}, u32[]{:S(2)}) copy-start(bf16[8,8,32,128]{3,2,1,0:T(8,128)(2,1)} %param.2) | copy-start | bytes 1572868
  66.5 9.2 %collective-permute-start = (bf16[32,8,128]{2,1,0:T(8,128)(2,1)S(1)}, bf16[32,8,128]{2,1,0:T(8,128)(2,1)S(1)}, u32[]{:S(2)}, u32[]{:S(2)}) collective-permute-start(bf16[32,8,128]{2,1,0:T(8,128)(2,1)S(1)} %get-tuple-element.9), channel_id=1, source_target_pairs={{0,64},{64,128},{128,192},{192,256},{256,320},{320,384},{384,448},... | collective-permute-start | bytes 196616 | tf_op jit(solution)/shard_map/ppermute | solution.py:175
  71.9 5.6 %collective-permute-start.1 = (bf16[32,8,128]{2,1,0:T(8,128)(2,1)S(1)}, bf16[32,8,128]{2,1,0:T(8,128)(2,1)S(1)}, u32[]{:S(2)}, u32[]{:S(2)}) collective-permute-start(bf16[32,8,128]{2,1,0:T(8,128)(2,1)S(1)} %get-tuple-element.10), channel_id=1, source_target_pairs={{64,0},{128,64},{192,128},{256,192},{320,256},{384,320},{448,384},... | collective-permute-start | bytes 196616 | tf_op jit(solution)/shard_map/ppermute | solution.py:176

commit v3 on v2

v3 whole, which is shorter than its diff:
```python
import jax
import jax.numpy as jnp
from jax import lax
from jax.experimental import pallas as pl
from jax.experimental.pallas import tpu as pltpu
from jax.sharding import PartitionSpec as P
ITERS=6
LIM=16<<20
GROUPS=[[(i + 60) % 64 for i in range(64)]]
RATE=0.12
F32=jnp.float32; BF=jnp.bfloat16
VM=pl.BlockSpec(memory_space=pltpu.VMEM); SM=pl.BlockSpec(memory_space=pltpu.SMEM); ANY=pl.BlockSpec(memory_space=pl.ANY)

def spread_kernel(off_ref, x_ref, o_ref, s_ref):
    sh = off_ref[0] & 511
    rr = sh >> 7
    lr = sh & 127
    for f in range(8):
        v = x_ref[f].astype(F32)
        s_ref[pl.ds(f, 256, stride=8), :] = v
    s_ref[2048:2088, :] = s_ref[0:40, :]
    lane = lax.broadcasted_iota(jnp.int32, (8,128), 1)
    keep = lane < 128 - lr
    back = (128 - lr) & 127
    def row(R):
        return pltpu.roll(s_ref[pl.ds(pl.multiple_of((rr+R)*8,8),8),:], back, 1)
    for j in range(0,64,2):
        rows=[row(4*j+i) for i in range(9)]
        o=[jnp.where(keep, rows[i], rows[i+1]) for i in range(8)]
        for c in range(4):
            o_ref[j,:,c*128:(c+1)*128]=o[c].astype(BF)
            o_ref[j+1,:,c*128:(c+1)*128]=o[4+c].astype(BF)

def spread(off,x):
    return pl.pallas_call(spread_kernel, out_shape=jax.ShapeDtypeStruct((64,8,512),BF),
        in_specs=[SM,VM], out_specs=VM, scratch_shapes=[pltpu.VMEM((2088,128),F32)], name="spread",
        compiler_params=pltpu.CompilerParams(vmem_limit_bytes=LIM),
        cost_estimate=pl.CostEstimate(flops=1<<20,bytes_accessed=1<<20,transcendentals=0))(off,x)

def shrink_kernel(m_ref, y_ref, a_ref, g_ref, w_ref, z_ref, gram_ref):
    n=512
    q=128
    eye=lax.broadcasted_iota(jnp.int32,(q,q),0)==lax.broadcasted_iota(jnp.int32,(q,q),1)
    squares=jnp.zeros((8,n),F32)
    trace=jnp.zeros((8,q),F32)
    for i in range(2):
        r=slice(i*256,(i+1)*256)
        gram=lax.dot_general(m_ref[r,:],m_ref[...],(((1,),(1,)),((),())),preferred_element_type=F32)
        gram_ref[r,:]=gram
        squares=squares+jnp.sum((gram*gram).reshape(32,8,n),axis=0)
        for k in range(2):
            d=gram[k*q:(k+1)*q,(2*i+k)*q:(2*i+k+1)*q]
            trace=trace+jnp.sum(jnp.where(eye,d,0.0).reshape(16,8,q),axis=0)
    scale=n/(jnp.sum(trace)+1e-6)
    norm=scale*jnp.sqrt(jnp.sum(squares))
    c=(1.0/(1.0+norm)).astype(BF).astype(F32)
    for i in range(4):
        for j in range(4):
            at=(slice(i*q,(i+1)*q),slice(j*q,(j+1)*q))
            g=gram_ref[at]*scale
            g_ref[at]=g.astype(BF)
            a=((g+jnp.where(eye,1.0,0.0)) if i==j else g).astype(BF)
            a_ref[at]=a
            z=-c*(a.astype(F32)*c).astype(BF).astype(F32)
            if i==j: z=z+jnp.where(eye,2.0*c,0.0)
            z_ref[0,i*q:(i+1)*q,j*q:(j+1)*q]=z.astype(BF)
    for k in range(ITERS-1):
        z=z_ref[k%2]
        w_ref[...]=jnp.dot(z,a_ref[...],preferred_element_type=F32).astype(BF)
        z_ref[(k+1)%2]=(2.0*z.astype(F32)-jnp.dot(w_ref[...],z,preferred_element_type=F32)).astype(BF)
    w_ref[...]=jnp.dot(z_ref[(ITERS-1)%2],g_ref[...],preferred_element_type=F32).astype(BF)
    y_ref[...]=jnp.dot(w_ref[...],m_ref[...],preferred_element_type=F32).astype(BF)

def shrink(m):
    sc=[pltpu.VMEM((512,512),BF)]*3+[pltpu.VMEM((2,512,512),BF),pltpu.VMEM((512,512),F32)]
    return pl.pallas_call(shrink_kernel,out_shape=jax.ShapeDtypeStruct((512,512),BF),in_specs=[VM],out_specs=VM,scratch_shapes=sc,name="shrink",
        compiler_params=pltpu.CompilerParams(vmem_limit_bytes=LIM),
        cost_estimate=pl.CostEstimate(flops=13*2*512**3,bytes_accessed=1<<20,transcendentals=0))(m)

def smooth_inside(off_ref, y_ref, out_ref, part_ref, t_ref, u_ref, o_ref, sem):
    sh = off_ref[0] & 511
    rr = sh >> 7
    lr = sh & 127
    lane = lax.broadcasted_iota(jnp.int32, (8,128), 1)
    keep = lane >= lr
    for j in [63]+list(range(64)):
        v = y_ref[j].astype(F32)
        base = 0 if j==63 else 4
        for c in range(4):
            val = pltpu.roll(v[:, c*128:(c+1)*128], lr, 1)
            if j==63: t_ref[260-4 + c] = val
            else: t_ref[4 + 4*j + c] = val
    t_ref[0:4] = t_ref[256:260]
    prev = t_ref[3 - rr]
    for R in range(256):
        cur = t_ref[R + 4 - rr]
        u_ref[R] = jnp.where(keep, cur, prev)
        prev = cur
    lo = lane > 0
    hi = lane < 127
    for p in range(8):
        for y in range(32):
            R = p*32+y
            c = u_ref[R]
            s = jnp.where(hi, pltpu.roll(c,127,1), 0.0) + jnp.where(lo, pltpu.roll(c,1,1), 0.0)
            if y>0: s = s + u_ref[R-1]
            if y<31: s = s + u_ref[R+1]
            if p>0: s = s + u_ref[R-32]
            if p<7: s = s + u_ref[R+32]
            val = (1.0-6.0*RATE)*c + RATE*s
            if p in (0,7): part_ref[0 if p==0 else 1, :, y, :] = val
            else: o_ref[p-1, :, y, :] = val
        if p not in (0,7):
            pltpu.make_async_copy(o_ref.at[p-1], out_ref.at[:,p], sem.at[p-1]).start()
    for p in range(6):
        pltpu.make_async_copy(o_ref.at[p], out_ref.at[:,p+1], sem.at[p]).wait()

def inner_kernel(off_ref, y_ref, out_in, part_in, out_ref, part_ref, t_ref, u_ref, o_ref, sem):
    @pl.when((lax.axis_index("space") & 1) == 0)
    def _():
        smooth_inside(off_ref, y_ref, out_ref, part_ref, t_ref, u_ref, o_ref, sem)
    @pl.when((lax.axis_index("space") & 1) == 1)
    def _():
        part_ref[...] = part_in[...]

INNER_SCRATCH=[pltpu.VMEM((260,8,128),F32),pltpu.VMEM((256,8,128),F32),pltpu.VMEM((6,8,32,128),F32),pltpu.SemaphoreType.DMA((6,))]
INNER_SHAPE=(jax.ShapeDtypeStruct((8,8,32,128),F32),jax.ShapeDtypeStruct((2,8,32,128),F32))

def inner(off,y,out,part):
    return pl.pallas_call(inner_kernel,out_shape=INNER_SHAPE,
        in_specs=[SM,VM,ANY,VM],out_specs=(ANY,VM),scratch_shapes=INNER_SCRATCH,name="inner",input_output_aliases={2:0,3:1},
        compiler_params=pltpu.CompilerParams(vmem_limit_bytes=LIM),
        cost_estimate=pl.CostEstimate(flops=1<<22,bytes_accessed=3<<19,transcendentals=0))(off,y,out,part)

def edges_kernel(off_ref, y_ref, far_ref, near_ref, out_ref, part_ref, e_ref, t_ref, u_ref, o_ref, sem):
    sh = off_ref[0] & 511
    rr = sh >> 7
    lr = sh & 127
    odd = (lax.axis_index("space") & 1) == 1
    lane = lax.broadcasted_iota(jnp.int32, (8,128), 1)
    keep = lane >= lr
    for k,j in enumerate([63]+list(range(8))+list(range(55,64))):
        v = y_ref[j].astype(F32)
        for c in range(4):
            e_ref[4*k + c] = pltpu.roll(v[:, c*128:(c+1)*128], lr, 1)
    prev0 = e_ref[3 - rr]
    prev1 = e_ref[39 - rr]
    for R in range(32):
        cur0 = e_ref[R + 4 - rr]
        cur1 = e_ref[R + 40 - rr]
        first = jnp.where(keep, cur0, prev0)
        last = jnp.where(keep, cur1, prev1)
        near_ref[R] = jnp.where(odd, first, last).astype(BF)
        far_ref[R] = jnp.where(odd, last, first).astype(BF)
        prev0 = cur0
        prev1 = cur1
    @pl.when((lax.axis_index("space") & 1) == 1)
    def _():
        smooth_inside(off_ref, y_ref, out_ref, part_ref, t_ref, u_ref, o_ref, sem)

def edges(off,y):
    s=jax.ShapeDtypeStruct((32,8,128),BF)
    return pl.pallas_call(edges_kernel,out_shape=(s,s)+INNER_SHAPE,in_specs=[SM,VM],out_specs=(VM,VM,ANY,VM),scratch_shapes=[pltpu.VMEM((72,8,128),F32)]+INNER_SCRATCH,name="edges",
        compiler_params=pltpu.CompilerParams(vmem_limit_bytes=LIM),
        cost_estimate=pl.CostEstimate(flops=1<<22,bytes_accessed=3<<19,transcendentals=0))(off,y)

def halo_kernel(far_ref, near_ref, part_ref, in_ref, out_ref, o_ref, sem):
    odd = (lax.axis_index("space") & 1) == 1
    for k in range(2):
        for y in range(32):
            n = near_ref[y].astype(F32)
            f = far_ref[y].astype(F32)
            h = jnp.where(odd, n, f) if k == 0 else jnp.where(odd, f, n)
            o_ref[k,:,y,:] = part_ref[k,:,y,:] + RATE*h
        pltpu.make_async_copy(o_ref.at[k], out_ref.at[:,7*k], sem.at[k]).start()
    for k in range(2):
        pltpu.make_async_copy(o_ref.at[k], out_ref.at[:,7*k], sem.at[k]).wait()

def halo(lo,hi,part,out):
    return pl.pallas_call(halo_kernel,out_shape=jax.ShapeDtypeStruct((8,8,32,128),F32),in_specs=[VM,VM,VM,ANY],out_specs=ANY,
        scratch_shapes=[pltpu.VMEM((2,8,32,128),F32),pltpu.SemaphoreType.DMA((2,))],input_output_aliases={3:0},name="halo",
        compiler_params=pltpu.CompilerParams(vmem_limit_bytes=LIM),
        cost_estimate=pl.CostEstimate(flops=1<<17,bytes_accessed=1<<19,transcendentals=0))(lo,hi,part,out)


def on_device(series, offsets):
    sent = spread(offsets, series.reshape(8, 256, 128))
    arrived = lax.all_to_all(sent, "frame", split_axis=0, concat_axis=0, tiled=True, axis_index_groups=GROUPS)
    shrunk = shrink(arrived.reshape(512, 512))
    back = lax.all_to_all(shrunk.reshape(64, 8, 512), "frame", split_axis=0, concat_axis=0, tiled=True, axis_index_groups=GROUPS)
    far, near, out, part = edges(offsets, back)
    count = lax.axis_size("space")
    across = [(i, i + 1) for i in range(1, count - 1, 2)]
    far_in = lax.ppermute(far, "space", across + [(j, i) for i, j in across])
    near_in = lax.ppermute(near, "space", [(i, i ^ 1) for i in range(count)])
    out, part = inner(offsets, back, out, part)
    return halo(far_in, near_in, part, out)


def solution(mesh):
    in_specs = (P("frame", "space", None, None), P("space"))
    out_specs = P("frame", "space", None, None)
    return jax.shard_map(
        on_device, mesh=mesh, in_specs=in_specs, out_specs=out_specs, check_vma=False
    )
```

time: 78.7 us -> 75 us (0.953)
  starting transfers between devices: 7.28 us -> 5.45 us
  Pallas kernels: 9.29 us -> 8.05 us
    ppermute x2, starting transfers between devices: 7.28 us -> 5.45 us  [the longest x1 3.53 us: on_device(): far_in = lax.ppermute(far, 'space', across + [(j, i) for i, j in across])]
    pallas_call x1, Pallas kernels: 5.89 us -> 4.53 us  [shrink(): pl.pallas_call(shrink_kernel, out_shape=jax.ShapeDtypeStruct((512, 512),...]
  transfers between devices with their start and end apart: 2 -> 2, of which waited for: 1 -> 1; matrix products, arithmetic and copies ran while one was open for 0% -> 0% of each run, Pallas kernels for 2% -> 0%
where the time goes in v3:
time: 75 us; the launch traced here: 74.7 us
  blocking collectives  58.4 us (78%)
  Pallas kernels  8.05 us (11%)
  starting transfers between devices  5.45 us (7%)
  waiting for transfers between devices  1.09 us (1%)
  local copies, waits for them, and re-layouts  1.03 us (1%)
    all_to_all x1, blocking collectives, on_device(): lax.all_to_all(sent, 'frame', split_axis=0, concat_axis=0, tiled=True, ax...  32.4 us
    all_to_all x1, blocking collectives, on_device(): lax.all_to_all(shrunk.reshape(64, 8, 512), 'frame', split_axis=0, concat_...  26 us
    pallas_call x1, Pallas kernels, shrink(): pl.pallas_call(shrink_kernel, out_shape=jax.ShapeDtypeStruct((512, 512),...  4.53 us
    ppermute x1, starting transfers between devices, on_device(): far_in = lax.ppermute(far, 'space', across + [(j, i) for i, j in across])  3.53 us
    pallas_call x1, Pallas kernels, edges(): pl.pallas_call(edges_kernel, out_shape=(s, s) + INNER_SHAPE, in_specs=[SM...  2.05 us
    ppermute x1, starting transfers between devices, on_device(): near_in = lax.ppermute(near, 'space', [(i, i ^ 1) for i in range(count)])  1.92 us
  transfers between devices with their start and end apart: 2, of which 1 were waited for; matrix products, arithmetic and copies ran while one was open for 0% of the time, Pallas kernels for 0%

profile of v3, /device:TPU:1, one launch (start us, length us, event | category | flops | bytes accessed | tf_op | source)
XLA Modules:
  0.0 74.7 jit_solution(8779545785146760466)
XLA Ops:
  0.7 0.0 copy-start
  0.7 1.0 %copy-done = bf16[8,8,32,128]{3,2,1,0:T(8,128)(2,1)S(1)} copy-done((bf16[8,8,32,128]{3,2,1,0:T(8,128)(2,1)S(1)}, bf16[8,8,32,128]{3,2,1,0:T(8,128)(2,1)}, u32[]{:S(2)}) %copy-start) | copy-done | bytes 524312
  1.7 0.4 spread.1
  2.1 32.4 %all_to_all.10 = bf16[64,8,512]{2,1,0:T(8,128)(2,1)S(1)} all-to-all(bf16[64,8,512]{2,1,0:T(8,128)(2,1)S(1)} %spread.1), channel_id=1, replica_groups={{60,61,62,63,0,1,2,3,4,5,6,7,8,9,10,11,12,13,14,15,16,17,18,19,20,21,22..., dimensions={0} | all-to-all | bytes 1048576 | tf_op jit(solution)/shard_map/all_to_all | solution.py:188
  34.5 4.5 %shrink.1 = bf16[512,512]{1,0:T(8,128)(2,1)S(1)} custom-call(bf16[512,512]{1,0:T(8,128)(2,1)S(1)} %bitcast.3), custom_call_target="tpu_custom_call" | custom-call | flops 3489660928 | bytes 1048576 | tf_op jit(solution)/shard_map/shrink/pallas_call | solution.py:76
  39.1 26.0 %all_to_all.11.y_ref = bf16[64,8,512]{2,1,0:T(8,128)(2,1)S(1)} all-to-all(bf16[64,8,512]{2,1,0:T(8,128)(2,1)S(1)} %bitcast.4), channel_id=1, replica_groups={{60,61,62,63,0,1,2,3,4,5,6,7,8,9,10,11,12,13,14,15,16,17,18,19,20,21,22..., dimensions={0} | all-to-all | bytes 1048576 | tf_op jit(solution)/shard_map/all_to_all | solution.py:190
  65.0 2.0 %edges.1 = (bf16[32,8,128]{2,1,0:T(8,128)(2,1)S(1)}, bf16[32,8,128]{2,1,0:T(8,128)(2,1)S(1)}, f32[8,8,32,128]{3,2,1,0:T(8,128)}, f32[2,8,32,128]{3,2,1,0:T(8,128)S(1)}) custom-call(s32[1]{0:T(128)S(6)} %copy.9.off_ref, bf16[64,8,512]{2,1,0:T(8,128)(2,1)S(1)} %all_to_all.11.y_ref), custom_call_target="tpu_custom_call" | custom-call | flops 4194304 | bytes 1572864 | tf_op jit(solution)/shard_map/edges/pallas_call | solution.py:163
  67.1 3.5 %collective-permute-start = (bf16[32,8,128]{2,1,0:T(8,128)(2,1)S(1)}, bf16[32,8,128]{2,1,0:T(8,128)(2,1)S(1)}, u32[]{:S(2)}, u32[]{:S(2)}) collective-permute-start(bf16[32,8,128]{2,1,0:T(8,128)(2,1)S(1)} %get-tuple-element.11), channel_id=1, source_target_pairs={{64,128},{192,256},{320,384},{128,64},{256,192},{384,320},{65,129}... | collective-permute-start | bytes 196616 | tf_op jit(solution)/shard_map/ppermute | solution.py:194
  70.6 1.9 %collective-permute-start.1 = (bf16[32,8,128]{2,1,0:T(8,128)(2,1)S(1)}, bf16[32,8,128]{2,1,0:T(8,128)(2,1)S(1)}, u32[]{:S(2)}, u32[]{:S(2)}) collective-permute-start(bf16[32,8,128]{2,1,0:T(8,128)(2,1)S(1)} %get-tuple-element.12), channel_id=1, source_target_pairs={{0,64},{64,0},{128,192},{192,128},{256,320},{320,256},{384,448},{4... | collective-permute-start | bytes 196616 | tf_op jit(solution)/shard_map/ppermute | solution.py:195
  72.5 0.1 inner.1
  72.7 0.0 collective-permute-done.far_ref
  72.7 1.1 %collective-permute-done.1.near_ref = bf16[32,8,128]{2,1,0:T(8,128)(2,1)S(1)} collective-permute-done((bf16[32,8,128]{2,1,0:T(8,128)(2,1)S(1)}, bf16[32,8,128]{2,1,0:T(8,128)(2,1)S(1)}, u32[]{:S(2)}, u32[]{:S(2)}) %collective-permute-start.1) | collective-permute-done | bytes 65568 | tf_op jit(solution)/shard_map/ppermute | solution.py:195
  73.8 1.0 %halo.1 = f32[8,8,32,128]{3,2,1,0:T(8,128)} custom-call(bf16[32,8,128]{2,1,0:T(8,128)(2,1)S(1)} %collective-permute-done.far_ref, bf16[32,8,128]{2,1,0:T(8,128)(2,1)S(1)} %collective-permute-done.1.near_ref, f32[2,8,32,128]{3,2,1,0:T(8,128)S(1)} %get-tuple-element.15.part_ref, f32[8,8,32,128]{3,2,1,0:T(8,128)} %get-tuple-element.16.in_ref), custom_call_target="tpu_custom_call", output_to_operand_aliasing={{}: (3, {})} | custom-call | flops 131072 | bytes 524288 | tf_op jit(solution)/shard_map/halo/pallas_call | solution.py:180
Async XLA Ops:
  0.7 1.0 %copy-start = (bf16[8,8,32,128]{3,2,1,0:T(8,128)(2,1)S(1)}, bf16[8,8,32,128]{3,2,1,0:T(8,128)(2,1)}, u32[]{:S(2)}) copy-start(bf16[8,8,32,128]{3,2,1,0:T(8,128)(2,1)} %param.2) | copy-start | bytes 1572868
  67.1 5.6 %collective-permute-start = (bf16[32,8,128]{2,1,0:T(8,128)(2,1)S(1)}, bf16[32,8,128]{2,1,0:T(8,128)(2,1)S(1)}, u32[]{:S(2)}, u32[]{:S(2)}) collective-permute-start(bf16[32,8,128]{2,1,0:T(8,128)(2,1)S(1)} %get-tuple-element.11), channel_id=1, source_target_pairs={{64,128},{192,256},{320,384},{128,64},{256,192},{384,320},{65,129}... | collective-permute-start | bytes 196616 | tf_op jit(solution)/shard_map/ppermute | solution.py:194
  70.6 3.1 %collective-permute-start.1 = (bf16[32,8,128]{2,1,0:T(8,128)(2,1)S(1)}, bf16[32,8,128]{2,1,0:T(8,128)(2,1)S(1)}, u32[]{:S(2)}, u32[]{:S(2)}) collective-permute-start(bf16[32,8,128]{2,1,0:T(8,128)(2,1)S(1)} %get-tuple-element.12), channel_id=1, source_target_pairs={{0,64},{64,0},{128,192},{192,128},{256,320},{320,256},{384,448},{4... | collective-permute-start | bytes 196616 | tf_op jit(solution)/shard_map/ppermute | solution.py:195

commit v4 on v3

--- a/solution.py
+++ b/solution.py
@@ -6,7 +6,11 @@
 from jax.sharding import PartitionSpec as P
 ITERS=6
 LIM=16<<20
-GROUPS=[[(i + 60) % 64 for i in range(64)]]
+ROOT=61
+def _steps(i):
+    ring=lambda a,b,n: min((a-b)%n,(b-a)%n)
+    return 4*(i//32 != ROOT//32) + ring(i//8%4, ROOT//8%4, 4) + ring(i%8, ROOT%8, 8)
+GROUPS=[[ROOT]+sorted([i for i in range(64) if i != ROOT], key=lambda i: (-_steps(i), i))]
 RATE=0.12
 F32=jnp.float32; BF=jnp.bfloat16
 VM=pl.BlockSpec(memory_space=pltpu.VMEM); SM=pl.BlockSpec(memory_space=pltpu.SMEM); ANY=pl.BlockSpec(memory_space=pl.ANY)
@@ -77,54 +81,63 @@
         compiler_params=pltpu.CompilerParams(vmem_limit_bytes=LIM),
         cost_estimate=pl.CostEstimate(flops=13*2*512**3,bytes_accessed=1<<20,transcendentals=0))(m)
 
-def smooth_inside(off_ref, y_ref, out_ref, part_ref, t_ref, u_ref, o_ref, sem):
+def smooth_inside(off_ref, y_ref, out_ref, part_ref, t_ref, u_ref, s_ref, o_ref, sem):
     sh = off_ref[0] & 511
     rr = sh >> 7
     lr = sh & 127
     lane = lax.broadcasted_iota(jnp.int32, (8,128), 1)
     keep = lane >= lr
-    for j in [63]+list(range(64)):
+    lo = lane > 0
+    hi = lane < 127
+    def fetch(j):
         v = y_ref[j].astype(F32)
-        base = 0 if j==63 else 4
         for c in range(4):
             val = pltpu.roll(v[:, c*128:(c+1)*128], lr, 1)
-            if j==63: t_ref[260-4 + c] = val
-            else: t_ref[4 + 4*j + c] = val
-    t_ref[0:4] = t_ref[256:260]
-    prev = t_ref[3 - rr]
-    for R in range(256):
-        cur = t_ref[R + 4 - rr]
-        u_ref[R] = jnp.where(keep, cur, prev)
-        prev = cur
-    lo = lane > 0
-    hi = lane < 127
+            t_ref[4 + 4*j + c] = val
+            if j == 63: t_ref[c] = val
+    def restore(p):
+        prev = t_ref[p*32 + 3 - rr]
+        for R in range(p*32, p*32+32):
+            cur = t_ref[R + 4 - rr]
+            u_ref[R] = jnp.where(keep, cur, prev)
+            prev = cur
+    fetch(63)
     for p in range(8):
-        for y in range(32):
-            R = p*32+y
-            c = u_ref[R]
-            s = jnp.where(hi, pltpu.roll(c,127,1), 0.0) + jnp.where(lo, pltpu.roll(c,1,1), 0.0)
-            if y>0: s = s + u_ref[R-1]
-            if y<31: s = s + u_ref[R+1]
-            if p>0: s = s + u_ref[R-32]
-            if p<7: s = s + u_ref[R+32]
-            val = (1.0-6.0*RATE)*c + RATE*s
-            if p in (0,7): part_ref[0 if p==0 else 1, :, y, :] = val
-            else: o_ref[p-1, :, y, :] = val
-        if p not in (0,7):
-            pltpu.make_async_copy(o_ref.at[p-1], out_ref.at[:,p], sem.at[p-1]).start()
-    for p in range(6):
-        pltpu.make_async_copy(o_ref.at[p], out_ref.at[:,p+1], sem.at[p]).wait()
-
-def inner_kernel(off_ref, y_ref, out_in, part_in, out_ref, part_ref, t_ref, u_ref, o_ref, sem):
+        for j in range(8*p, 8*p+8):
+            if j != 63: fetch(j)
+        restore(p)
+        if p > 0: smooth(p-1, u_ref, s_ref, o_ref, out_ref, part_ref, sem, lo, hi)
+    smooth(7, u_ref, s_ref, o_ref, out_ref, part_ref, sem, lo, hi)
+    for p in range(1, 7):
+        pltpu.make_async_copy(o_ref.at[p-1], out_ref.at[:,p], sem.at[p-1]).wait()
+
+def smooth(p, u_ref, s_ref, o_ref, out_ref, part_ref, sem, lo, hi):
+    for y in range(32):
+        R = p*32+y
+        c = u_ref[R]
+        s = jnp.where(hi, pltpu.roll(c,127,1), 0.0) + jnp.where(lo, pltpu.roll(c,1,1), 0.0)
+        if y>0: s = s + u_ref[R-1]
+        if y<31: s = s + u_ref[R+1]
+        if p>0: s = s + u_ref[R-32]
+        if p<7: s = s + u_ref[R+32]
+        val = (1.0-6.0*RATE)*c + RATE*s
+        if p in (0,7): part_ref[p//7, y*8:(y+1)*8, :] = val
+        else: s_ref[R*8:(R+1)*8, :] = val
+    if p not in (0,7):
+        for f in range(8):
+            o_ref[p-1, f] = s_ref[pl.ds(p*256+f, 32, stride=8), :]
+        pltpu.make_async_copy(o_ref.at[p-1], out_ref.at[:,p], sem.at[p-1]).start()
+
+def inner_kernel(off_ref, y_ref, out_in, part_in, out_ref, part_ref, t_ref, u_ref, s_ref, o_ref, sem):
     @pl.when((lax.axis_index("space") & 1) == 0)
     def _():
-        smooth_inside(off_ref, y_ref, out_ref, part_ref, t_ref, u_ref, o_ref, sem)
+        smooth_inside(off_ref, y_ref, out_ref, part_ref, t_ref, u_ref, s_ref, o_ref, sem)
     @pl.when((lax.axis_index("space") & 1) == 1)
     def _():
         part_ref[...] = part_in[...]
 
-INNER_SCRATCH=[pltpu.VMEM((260,8,128),F32),pltpu.VMEM((256,8,128),F32),pltpu.VMEM((6,8,32,128),F32),pltpu.SemaphoreType.DMA((6,))]
-INNER_SHAPE=(jax.ShapeDtypeStruct((8,8,32,128),F32),jax.ShapeDtypeStruct((2,8,32,128),F32))
+INNER_SCRATCH=[pltpu.VMEM((260,8,128),F32),pltpu.VMEM((256,8,128),F32),pltpu.VMEM((2048,128),F32),pltpu.VMEM((6,8,32,128),F32),pltpu.SemaphoreType.DMA((6,))]
+INNER_SHAPE=(jax.ShapeDtypeStruct((8,8,32,128),F32),jax.ShapeDtypeStruct((2,256,128),F32))
 
 def inner(off,y,out,part):
     return pl.pallas_call(inner_kernel,out_shape=INNER_SHAPE,
@@ -132,7 +145,7 @@
         compiler_params=pltpu.CompilerParams(vmem_limit_bytes=LIM),
         cost_estimate=pl.CostEstimate(flops=1<<22,bytes_accessed=3<<19,transcendentals=0))(off,y,out,part)
 
-def edges_kernel(off_ref, y_ref, far_ref, near_ref, out_ref, part_ref, e_ref, t_ref, u_ref, o_ref, sem):
+def edges_kernel(off_ref, y_ref, far_ref, near_ref, out_ref, part_ref, e_ref, t_ref, u_ref, s_ref, o_ref, sem):
     sh = off_ref[0] & 511
     rr = sh >> 7
     lr = sh & 127
@@ -156,7 +169,7 @@
         prev1 = cur1
     @pl.when((lax.axis_index("space") & 1) == 1)
     def _():
-        smooth_inside(off_ref, y_ref, out_ref, part_ref, t_ref, u_ref, o_ref, sem)
+        smooth_inside(off_ref, y_ref, out_ref, part_ref, t_ref, u_ref, s_ref, o_ref, sem)
 
 def edges(off,y):
     s=jax.ShapeDtypeStruct((32,8,128),BF)
@@ -164,23 +177,25 @@
         compiler_params=pltpu.CompilerParams(vmem_limit_bytes=LIM),
         cost_estimate=pl.CostEstimate(flops=1<<22,bytes_accessed=3<<19,transcendentals=0))(off,y)
 
-def halo_kernel(far_ref, near_ref, part_ref, in_ref, out_ref, o_ref, sem):
+def halo_kernel(far_ref, near_ref, part_ref, in_ref, out_ref, s_ref, o_ref, sem):
     odd = (lax.axis_index("space") & 1) == 1
     for k in range(2):
         for y in range(32):
             n = near_ref[y].astype(F32)
             f = far_ref[y].astype(F32)
             h = jnp.where(odd, n, f) if k == 0 else jnp.where(odd, f, n)
-            o_ref[k,:,y,:] = part_ref[k,:,y,:] + RATE*h
+            s_ref[k, y*8:(y+1)*8, :] = part_ref[k, y*8:(y+1)*8, :] + RATE*h
+        for f in range(8):
+            o_ref[k, f] = s_ref[k, pl.ds(f, 32, stride=8), :]
         pltpu.make_async_copy(o_ref.at[k], out_ref.at[:,7*k], sem.at[k]).start()
     for k in range(2):
         pltpu.make_async_copy(o_ref.at[k], out_ref.at[:,7*k], sem.at[k]).wait()
 
-def halo(lo,hi,part,out):
+def halo(far,near,part,out):
     return pl.pallas_call(halo_kernel,out_shape=jax.ShapeDtypeStruct((8,8,32,128),F32),in_specs=[VM,VM,VM,ANY],out_specs=ANY,
-        scratch_shapes=[pltpu.VMEM((2,8,32,128),F32),pltpu.SemaphoreType.DMA((2,))],input_output_aliases={3:0},name="halo",
-        compiler_params=pltpu.CompilerParams(vmem_limit_bytes=LIM),
-        cost_estimate=pl.CostEstimate(flops=1<<17,bytes_accessed=1<<19,transcendentals=0))(lo,hi,part,out)
+        scratch_shapes=[pltpu.VMEM((2,256,128),F32),pltpu.VMEM((2,8,32,128),F32),pltpu.SemaphoreType.DMA((2,))],input_output_aliases={3:0},name="halo",
+        compiler_params=pltpu.CompilerParams(vmem_limit_bytes=LIM),
+        cost_estimate=pl.CostEstimate(flops=1<<17,bytes_accessed=1<<19,transcendentals=0))(far,near,part,out)
 
 
 def on_device(series, offsets):

time: 75 us -> 74.2 us (0.989)
    all_to_all x1, blocking collectives: 26 us -> 25.1 us  [on_device(): lax.all_to_all(shrunk.reshape(64, 8, 512), 'frame', split_axis=0, concat_...]
where the time goes in v4:
time: 74.2 us; the launch traced here: 73.9 us
  blocking collectives  57.8 us (78%)
  Pallas kernels  7.49 us (10%)
  starting transfers between devices  5.81 us (8%)
  waiting for transfers between devices  1.1 us (1%)
  local copies, waits for them, and re-layouts  1.03 us (1%)
    all_to_all x1, blocking collectives, on_device(): lax.all_to_all(sent, 'frame', split_axis=0, concat_axis=0, tiled=True, ax...  32.7 us
    all_to_all x1, blocking collectives, on_device(): lax.all_to_all(shrunk.reshape(64, 8, 512), 'frame', split_axis=0, concat_...  25.1 us
    pallas_call x1, Pallas kernels, shrink(): pl.pallas_call(shrink_kernel, out_shape=jax.ShapeDtypeStruct((512, 512),...  4.53 us
    ppermute x1, starting transfers between devices, on_device(): far_in = lax.ppermute(far, 'space', across + [(j, i) for i, j in across])  3.89 us
    ppermute x1, starting transfers between devices, on_device(): near_in = lax.ppermute(near, 'space', [(i, i ^ 1) for i in range(count)])  1.92 us
    pallas_call x1, Pallas kernels, edges(): pl.pallas_call(edges_kernel, out_shape=(s, s) + INNER_SHAPE, in_specs=[SM...  1.7 us
  transfers between devices with their start and end apart: 2, of which 1 were waited for; matrix products, arithmetic and copies ran while one was open for 0% of the time, Pallas kernels for 0%

profile of v4, /device:TPU:1, one launch (start us, length us, event | category | flops | bytes accessed | tf_op | source)
XLA Modules:
  0.0 73.9 jit_solution(8278095286013712341)
XLA Ops:
  0.7 0.0 copy-start
  0.7 1.0 %copy-done = bf16[8,8,32,128]{3,2,1,0:T(8,128)(2,1)S(1)} copy-done((bf16[8,8,32,128]{3,2,1,0:T(8,128)(2,1)S(1)}, bf16[8,8,32,128]{3,2,1,0:T(8,128)(2,1)}, u32[]{:S(2)}) %copy-start) | copy-done | bytes 524312
  1.7 0.4 spread.1
  2.1 32.7 %all_to_all.10 = bf16[64,8,512]{2,1,0:T(8,128)(2,1)S(1)} all-to-all(bf16[64,8,512]{2,1,0:T(8,128)(2,1)S(1)} %spread.1), channel_id=1, replica_groups={{61,9,1,8,10,17,0,2,11,15,16,18,25,3,7,12,14,19,23,24,26,4,6,13,20,22,2..., dimensions={0} | all-to-all | bytes 1048576 | tf_op jit(solution)/shard_map/all_to_all | solution.py:203
  34.7 4.5 %shrink.1 = bf16[512,512]{1,0:T(8,128)(2,1)S(1)} custom-call(bf16[512,512]{1,0:T(8,128)(2,1)S(1)} %bitcast.3), custom_call_target="tpu_custom_call" | custom-call | flops 3489660928 | bytes 1048576 | tf_op jit(solution)/shard_map/shrink/pallas_call | solution.py:80
  39.3 25.1 %all_to_all.11.y_ref = bf16[64,8,512]{2,1,0:T(8,128)(2,1)S(1)} all-to-all(bf16[64,8,512]{2,1,0:T(8,128)(2,1)S(1)} %bitcast.4), channel_id=1, replica_groups={{61,9,1,8,10,17,0,2,11,15,16,18,25,3,7,12,14,19,23,24,26,4,6,13,20,22,2..., dimensions={0} | all-to-all | bytes 1048576 | tf_op jit(solution)/shard_map/all_to_all | solution.py:205
  64.4 1.7 %edges.1 = (bf16[32,8,128]{2,1,0:T(8,128)(2,1)S(1)}, bf16[32,8,128]{2,1,0:T(8,128)(2,1)S(1)}, f32[8,8,32,128]{3,2,1,0:T(8,128)}, f32[2,256,128]{2,1,0:T(8,128)S(1)}) custom-call(s32[1]{0:T(128)S(6)} %copy.9.off_ref, bf16[64,8,512]{2,1,0:T(8,128)(2,1)S(1)} %all_to_all.11.y_ref), custom_call_target="tpu_custom_call" | custom-call | flops 4194304 | bytes 1572864 | tf_op jit(solution)/shard_map/edges/pallas_call | solution.py:176
  66.1 3.9 %collective-permute-start = (bf16[32,8,128]{2,1,0:T(8,128)(2,1)S(1)}, bf16[32,8,128]{2,1,0:T(8,128)(2,1)S(1)}, u32[]{:S(2)}, u32[]{:S(2)}) collective-permute-start(bf16[32,8,128]{2,1,0:T(8,128)(2,1)S(1)} %get-tuple-element.11), channel_id=1, source_target_pairs={{64,128},{192,256},{320,384},{128,64},{256,192},{384,320},{65,129}... | collective-permute-start | bytes 196616 | tf_op jit(solution)/shard_map/ppermute | solution.py:209
  70.0 1.9 %collective-permute-start.1 = (bf16[32,8,128]{2,1,0:T(8,128)(2,1)S(1)}, bf16[32,8,128]{2,1,0:T(8,128)(2,1)S(1)}, u32[]{:S(2)}, u32[]{:S(2)}) collective-permute-start(bf16[32,8,128]{2,1,0:T(8,128)(2,1)S(1)} %get-tuple-element.12), channel_id=1, source_target_pairs={{0,64},{64,0},{128,192},{192,128},{256,320},{320,256},{384,448},{4... | collective-permute-start | bytes 196616 | tf_op jit(solution)/shard_map/ppermute | solution.py:210
  71.9 0.1 inner.1
  72.0 0.0 collective-permute-done.far_ref
  72.0 1.1 %collective-permute-done.1.near_ref = bf16[32,8,128]{2,1,0:T(8,128)(2,1)S(1)} collective-permute-done((bf16[32,8,128]{2,1,0:T(8,128)(2,1)S(1)}, bf16[32,8,128]{2,1,0:T(8,128)(2,1)S(1)}, u32[]{:S(2)}, u32[]{:S(2)}) %collective-permute-start.1) | collective-permute-done | bytes 65568 | tf_op jit(solution)/shard_map/ppermute | solution.py:210
  73.1 0.8 %halo.1 = f32[8,8,32,128]{3,2,1,0:T(8,128)} custom-call(bf16[32,8,128]{2,1,0:T(8,128)(2,1)S(1)} %collective-permute-done.far_ref, bf16[32,8,128]{2,1,0:T(8,128)(2,1)S(1)} %collective-permute-done.1.near_ref, f32[2,256,128]{2,1,0:T(8,128)S(1)} %get-tuple-element.15.part_ref, f32[8,8,32,128]{3,2,1,0:T(8,128)} %get-tuple-element.16.in_ref), custom_call_target="tpu_custom_call", output_to_operand_aliasing={{}: (3, {})} | custom-call | flops 131072 | bytes 524288 | tf_op jit(solution)/shard_map/halo/pallas_call | solution.py:195
Async XLA Ops:
  0.7 1.0 %copy-start = (bf16[8,8,32,128]{3,2,1,0:T(8,128)(2,1)S(1)}, bf16[8,8,32,128]{3,2,1,0:T(8,128)(2,1)}, u32[]{:S(2)}) copy-start(bf16[8,8,32,128]{3,2,1,0:T(8,128)(2,1)} %param.2) | copy-start | bytes 1572868
  66.1 5.9 %collective-permute-start = (bf16[32,8,128]{2,1,0:T(8,128)(2,1)S(1)}, bf16[32,8,128]{2,1,0:T(8,128)(2,1)S(1)}, u32[]{:S(2)}, u32[]{:S(2)}) collective-permute-start(bf16[32,8,128]{2,1,0:T(8,128)(2,1)S(1)} %get-tuple-element.11), channel_id=1, source_target_pairs={{64,128},{192,256},{320,384},{128,64},{256,192},{384,320},{65,129}... | collective-permute-start | bytes 196616 | tf_op jit(solution)/shard_map/ppermute | solution.py:209
  70.0 3.1 %collective-permute-start.1 = (bf16[32,8,128]{2,1,0:T(8,128)(2,1)S(1)}, bf16[32,8,128]{2,1,0:T(8,128)(2,1)S(1)}, u32[]{:S(2)}, u32[]{:S(2)}) collective-permute-start(bf16[32,8,128]{2,1,0:T(8,128)(2,1)S(1)} %get-tuple-element.12), channel_id=1, source_target_pairs={{0,64},{64,0},{128,192},{192,128},{256,320},{320,256},{384,448},{4... | collective-permute-start | bytes 196616 | tf_op jit(solution)/shard_map/ppermute | solution.py:210

commit v5 on v4

--- a/solution.py
+++ b/solution.py
@@ -1,3 +1,4 @@
+import functools
 import jax
 import jax.numpy as jnp
 from jax import lax
@@ -177,25 +178,22 @@
         compiler_params=pltpu.CompilerParams(vmem_limit_bytes=LIM),
         cost_estimate=pl.CostEstimate(flops=1<<22,bytes_accessed=3<<19,transcendentals=0))(off,y)
 
-def halo_kernel(far_ref, near_ref, part_ref, in_ref, out_ref, s_ref, o_ref, sem):
-    odd = (lax.axis_index("space") & 1) == 1
-    for k in range(2):
-        for y in range(32):
-            n = near_ref[y].astype(F32)
-            f = far_ref[y].astype(F32)
-            h = jnp.where(odd, n, f) if k == 0 else jnp.where(odd, f, n)
-            s_ref[k, y*8:(y+1)*8, :] = part_ref[k, y*8:(y+1)*8, :] + RATE*h
-        for f in range(8):
-            o_ref[k, f] = s_ref[k, pl.ds(f, 32, stride=8), :]
-        pltpu.make_async_copy(o_ref.at[k], out_ref.at[:,7*k], sem.at[k]).start()
-    for k in range(2):
-        pltpu.make_async_copy(o_ref.at[k], out_ref.at[:,7*k], sem.at[k]).wait()
-
-def halo(far,near,part,out):
-    return pl.pallas_call(halo_kernel,out_shape=jax.ShapeDtypeStruct((8,8,32,128),F32),in_specs=[VM,VM,VM,ANY],out_specs=ANY,
-        scratch_shapes=[pltpu.VMEM((2,256,128),F32),pltpu.VMEM((2,8,32,128),F32),pltpu.SemaphoreType.DMA((2,))],input_output_aliases={3:0},name="halo",
-        compiler_params=pltpu.CompilerParams(vmem_limit_bytes=LIM),
-        cost_estimate=pl.CostEstimate(flops=1<<17,bytes_accessed=1<<19,transcendentals=0))(far,near,part,out)
+def plane_kernel(far, h_ref, part_ref, in_ref, out_ref, s_ref, o_ref, sem):
+    odd = lax.axis_index("space") & 1
+    k = odd if far else 1 - odd
+    for y in range(32):
+        s_ref[y*8:(y+1)*8, :] = part_ref[k, y*8:(y+1)*8, :] + RATE*h_ref[y].astype(F32)
+    for f in range(8):
+        o_ref[f] = s_ref[pl.ds(f, 32, stride=8), :]
+    copy = pltpu.make_async_copy(o_ref, out_ref.at[:, 7*k], sem)
+    copy.start()
+    copy.wait()
+
+def add_plane(far,h,part,out):
+    return pl.pallas_call(functools.partial(plane_kernel,far),out_shape=jax.ShapeDtypeStruct((8,8,32,128),F32),in_specs=[VM,VM,ANY],out_specs=ANY,
+        scratch_shapes=[pltpu.VMEM((256,128),F32),pltpu.VMEM((8,32,128),F32),pltpu.SemaphoreType.DMA],input_output_aliases={2:0},name="far_plane" if far else "near_plane",
+        compiler_params=pltpu.CompilerParams(vmem_limit_bytes=LIM),
+        cost_estimate=pl.CostEstimate(flops=1<<16,bytes_accessed=1<<18,transcendentals=0))(h,part,out)
 
 
 def on_device(series, offsets):
@@ -207,9 +205,11 @@
     count = lax.axis_size("space")
     across = [(i, i + 1) for i in range(1, count - 1, 2)]
     far_in = lax.ppermute(far, "space", across + [(j, i) for i, j in across])
+    out, part = inner(offsets, back, out, part)
+    near, part = lax.optimization_barrier((near, part))
     near_in = lax.ppermute(near, "space", [(i, i ^ 1) for i in range(count)])
-    out, part = inner(offsets, back, out, part)
-    return halo(far_in, near_in, part, out)
+    out = add_plane(True, far_in, part, out)
+    return add_plane(False, near_in, part, out)
 
 
 def solution(mesh):

time: 74.2 us -> 74.2 us (level)
  transfers between devices with their start and end apart: 2 -> 2, of which waited for: 1 -> 1; matrix products, arithmetic and copies ran while one was open for 0% -> 0% of each run, Pallas kernels for 0% -> 1%
where the time goes in v5:
time: 74.2 us; the launch traced here: 74 us
  blocking collectives  57.8 us (78%)
  Pallas kernels  8.14 us (11%)
  starting transfers between devices  5.8 us (8%)
  local copies, waits for them, and re-layouts  1.03 us (1%)
    all_to_all x1, blocking collectives, on_device(): lax.all_to_all(sent, 'frame', split_axis=0, concat_axis=0, tiled=True, ax...  32.7 us
    all_to_all x1, blocking collectives, on_device(): lax.all_to_all(shrunk.reshape(64, 8, 512), 'frame', split_axis=0, concat_...  25.1 us
    pallas_call x1, Pallas kernels, shrink(): pl.pallas_call(shrink_kernel, out_shape=jax.ShapeDtypeStruct((512, 512),...  4.53 us
    ppermute x1, starting transfers between devices, on_device(): far_in = lax.ppermute(far, 'space', across + [(j, i) for i, j in across])  3.88 us
    ppermute x1, starting transfers between devices, on_device(): near_in = lax.ppermute(near, 'space', [(i, i ^ 1) for i in range(count)])  1.92 us
    pallas_call x1, Pallas kernels, edges(): pl.pallas_call(edges_kernel, out_shape=(s, s) + INNER_SHAPE, in_specs=[SM...  1.7 us
  transfers between devices with their start and end apart: 2, of which 1 were waited for; matrix products, arithmetic and copies ran while one was open for 0% of the time, Pallas kernels for 1%

profile of v5, /device:TPU:1, one launch (start us, length us, event | category | flops | bytes accessed | tf_op | source)
XLA Modules:
  0.0 74.0 jit_solution(4561105584919736079)
XLA Ops:
  0.7 0.0 copy-start
  0.7 1.0 %copy-done = bf16[8,8,32,128]{3,2,1,0:T(8,128)(2,1)S(1)} copy-done((bf16[8,8,32,128]{3,2,1,0:T(8,128)(2,1)S(1)}, bf16[8,8,32,128]{3,2,1,0:T(8,128)(2,1)}, u32[]{:S(2)}) %copy-start) | copy-done | bytes 524312
  1.7 0.4 spread.1
  2.1 32.7 %all_to_all.10 = bf16[64,8,512]{2,1,0:T(8,128)(2,1)S(1)} all-to-all(bf16[64,8,512]{2,1,0:T(8,128)(2,1)S(1)} %spread.1), channel_id=1, replica_groups={{61,9,1,8,10,17,0,2,11,15,16,18,25,3,7,12,14,19,23,24,26,4,6,13,20,22,2..., dimensions={0} | all-to-all | bytes 1048576 | tf_op jit(solution)/shard_map/all_to_all | solution.py:201
  34.7 4.5 %shrink.1 = bf16[512,512]{1,0:T(8,128)(2,1)S(1)} custom-call(bf16[512,512]{1,0:T(8,128)(2,1)S(1)} %bitcast.3), custom_call_target="tpu_custom_call" | custom-call | flops 3489660928 | bytes 1048576 | tf_op jit(solution)/shard_map/shrink/pallas_call | solution.py:81
  39.3 25.1 %all_to_all.11.y_ref = bf16[64,8,512]{2,1,0:T(8,128)(2,1)S(1)} all-to-all(bf16[64,8,512]{2,1,0:T(8,128)(2,1)S(1)} %bitcast.4), channel_id=1, replica_groups={{61,9,1,8,10,17,0,2,11,15,16,18,25,3,7,12,14,19,23,24,26,4,6,13,20,22,2..., dimensions={0} | all-to-all | bytes 1048576 | tf_op jit(solution)/shard_map/all_to_all | solution.py:203
  64.4 1.7 %edges.1 = (bf16[32,8,128]{2,1,0:T(8,128)(2,1)S(1)}, bf16[32,8,128]{2,1,0:T(8,128)(2,1)S(1)}, f32[8,8,32,128]{3,2,1,0:T(8,128)}, f32[2,256,128]{2,1,0:T(8,128)S(1)}) custom-call(s32[1]{0:T(128)S(6)} %copy.11.off_ref, bf16[64,8,512]{2,1,0:T(8,128)(2,1)S(1)} %all_to_all.11.y_ref), custom_call_target="tpu_custom_call" | custom-call | flops 4194304 | bytes 1572864 | tf_op jit(solution)/shard_map/edges/pallas_call | solution.py:177
  66.1 3.9 %collective-permute-start.1 = (bf16[32,8,128]{2,1,0:T(8,128)(2,1)S(1)}, bf16[32,8,128]{2,1,0:T(8,128)(2,1)S(1)}, u32[]{:S(2)}, u32[]{:S(2)}) collective-permute-start(bf16[32,8,128]{2,1,0:T(8,128)(2,1)S(1)} %get-tuple-element.19), channel_id=1, source_target_pairs={{64,128},{192,256},{320,384},{128,64},{256,192},{384,320},{65,129}... | collective-permute-start | bytes 196616 | tf_op jit(solution)/shard_map/ppermute | solution.py:207
  70.0 0.1 inner.1
  70.1 1.9 %collective-permute-start = (bf16[32,8,128]{2,1,0:T(8,128)(2,1)S(1)}, bf16[32,8,128]{2,1,0:T(8,128)(2,1)S(1)}, u32[]{:S(2)}, u32[]{:S(2)}) collective-permute-start(bf16[32,8,128]{2,1,0:T(8,128)(2,1)S(1)} %get-tuple-element.17), channel_id=1, source_target_pairs={{0,64},{64,0},{128,192},{192,128},{256,320},{320,256},{384,448},{4... | collective-permute-start | bytes 196616 | tf_op jit(solution)/shard_map/ppermute | solution.py:210
  72.0 0.0 collective-permute-done.1.h_ref
  72.0 0.7 far_plane.1.in_ref
  72.8 0.5 collective-permute-done.h_ref
  73.2 0.7 near_plane.1
Async XLA Ops:
  0.7 1.0 %copy-start = (bf16[8,8,32,128]{3,2,1,0:T(8,128)(2,1)S(1)}, bf16[8,8,32,128]{3,2,1,0:T(8,128)(2,1)}, u32[]{:S(2)}) copy-start(bf16[8,8,32,128]{3,2,1,0:T(8,128)(2,1)} %param.2) | copy-start | bytes 1572868
  66.1 5.9 %collective-permute-start.1 = (bf16[32,8,128]{2,1,0:T(8,128)(2,1)S(1)}, bf16[32,8,128]{2,1,0:T(8,128)(2,1)S(1)}, u32[]{:S(2)}, u32[]{:S(2)}) collective-permute-start(bf16[32,8,128]{2,1,0:T(8,128)(2,1)S(1)} %get-tuple-element.19), channel_id=1, source_target_pairs={{64,128},{192,256},{320,384},{128,64},{256,192},{384,320},{65,129}... | collective-permute-start | bytes 196616 | tf_op jit(solution)/shard_map/ppermute | solution.py:207
  70.1 3.1 %collective-permute-start = (bf16[32,8,128]{2,1,0:T(8,128)(2,1)S(1)}, bf16[32,8,128]{2,1,0:T(8,128)(2,1)S(1)}, u32[]{:S(2)}, u32[]{:S(2)}) collective-permute-start(bf16[32,8,128]{2,1,0:T(8,128)(2,1)S(1)} %get-tuple-element.17), channel_id=1, source_target_pairs={{0,64},{64,0},{128,192},{192,128},{256,320},{320,256},{384,448},{4... | collective-permute-start | bytes 196616 | tf_op jit(solution)/shard_map/ppermute | solution.py:210
